TPU v7x, 256 devices: a whole 4x4x8 slice. The times are simulated.
256 devices in a mesh: shard: 8 (over z_lo, x), tensor: 4 (over z_hi), section: 8 (over y, core).
Axes of the slice: x: 4, y: 4, z: 8 (z_hi: 4, z_lo: 2; z = z_hi * 2 + z_lo), core: 2. Of those that a mesh axis runs over, the one named last changes fastest.
Arguments:
- activations: bfloat16 [8, 2048, 2304], P(None, 'shard', ('tensor', 'section')), may hold values from -6 to 6
- router_grad: bfloat16 [8, 2048], P(None, 'shard'), may hold values from -6 to 6
- token_ids: int32 [2048], P('shard'), may hold values from 0 to 8191
- norm_terms: bfloat16 [2, 2048, 2304], P(None, 'shard', ('tensor', 'section'))
- old_factors: float32 [8, 2304, 2304], P('shard', 'tensor', 'section'), as said below
- old_router_factor: float32 [8, 8], replicated, as said below
- old_norm_diag: float32 [2, 2304], P(None, ('tensor', 'section')), may hold values from 0.5 to 5
- old_embed_diag: float32 [8192], P('tensor'), may hold values from 0.05 to 0.5
Outputs:
- precond_attn: float32 [4, 2304, 2304], P(None, 'tensor', 'section')
- precond_router: float32 [8, 2304], P(None, 'tensor')
- precond_norms: float32 [2, 2304], P(None, ('tensor', 'section'))
- precond_embed: float32 [8192, 2304], P('tensor', 'section')
Inputs may be any that keep to these rules, and one draw needn't show every extreme that they name: `old_factors`: each matrix is symmetric with a positive diagonal. `old_router_factor`: symmetric with a positive diagonal.
All inputs are finite; a program needn't handle non-finite values.
Results may differ from a plain program's by a relative error of at most 0.0083.
Values may be sent and summed in bfloat16 or wider, within the bound.
A program may use at most 64 MiB of HBM per device.

v0:
```python
import math

import jax
import jax.numpy as jnp
from jax import lax
from jax.sharding import PartitionSpec as P

D = 2304
EXPERTS = 8
VOCAB = 8192


factor_decay = 0.5
damping = 0.01
learning_rate = 0.05


def local_inverse(matrix):
    width = matrix.shape[0]
    trace = jnp.sum(jnp.diagonal(matrix))
    factor_scale = width / (3.0 * trace)
    identity = jnp.eye(width, dtype=jnp.float32)
    matrix_low = lax.optimization_barrier(matrix.astype(jnp.bfloat16))
    first = 2.0 * factor_scale * identity - factor_scale * factor_scale * matrix_low.astype(
        jnp.float32
    )
    first_low = first.astype(jnp.bfloat16)
    image = jnp.dot(matrix_low, first_low, preferred_element_type=jnp.float32).astype(jnp.bfloat16)
    product = jnp.dot(first_low, image, preferred_element_type=jnp.float32)
    return (2.0 * first - product).astype(jnp.bfloat16)


def fold_with(columns, piece):
    return jnp.einsum("kij,kjl->kil", piece, columns, preferred_element_type=jnp.float32)


def per_device(
    activations,
    router_grad,
    token_ids,
    norm_terms,
    old_factors,
    old_router_factor,
    old_norm_diag,
    old_embed_diag,
):
    n_tensor = lax.axis_size("tensor")
    n_section = lax.axis_size("section")
    n_shard = lax.axis_size("shard")
    tensor_rank = lax.axis_index("tensor")
    section_rank = lax.axis_index("section")
    row_block = D // n_tensor
    col_block = D // n_section
    tokens_all = activations.shape[1] * n_shard
    row_start = tensor_rank * row_block
    col_start = section_rank * col_block

    def collect(carry, piece):
        whole = lax.all_gather(piece, ("tensor", "section"), axis=1, tiled=True)
        rows_part = lax.dynamic_slice_in_dim(whole, row_start, row_block, 1)
        cols_part = lax.dynamic_slice_in_dim(whole, col_start, col_block, 1)
        return (carry, (rows_part, cols_part))

    unused_carry, (row_parts, col_parts) = lax.scan(collect, jnp.int32(0), activations)
    partial_value = jnp.einsum(
        "mnr,mnc->mrc", row_parts, col_parts, preferred_element_type=jnp.float32
    )
    fresh = lax.psum_scatter(partial_value, "shard", scatter_dimension=0, tiled=True) / tokens_all
    row_index = lax.broadcasted_iota(jnp.int32, (row_block, col_block), 0) + row_start
    col_index = lax.broadcasted_iota(jnp.int32, (row_block, col_block), 1) + col_start
    eye_block = (row_index == col_index).astype(jnp.float32)
    matrix = factor_decay * old_factors + (1.0 - factor_decay) * fresh + damping * eye_block
    diag_part = jnp.sum(matrix * eye_block, axis=(1, 2))
    trace = lax.psum(diag_part, ("tensor", "section"))
    factor_scale = (D / (3.0 * trace))[:, None, None]
    matrix_low = lax.optimization_barrier(matrix.astype(jnp.bfloat16))
    first = 2.0 * factor_scale * eye_block - factor_scale * factor_scale * matrix_low.astype(
        jnp.float32
    )
    first_low = first.astype(jnp.bfloat16)
    first_cols = lax.all_gather(first_low, "tensor", axis=1, tiled=True)
    image = fold_with(first_cols, lax.all_gather(matrix_low, "section", axis=2, tiled=True))
    image_cols = lax.all_gather(image.astype(jnp.bfloat16), "tensor", axis=1, tiled=True)
    product = fold_with(image_cols, lax.all_gather(first_low, "section", axis=2, tiled=True))
    inverse_low = (2.0 * first - product).astype(jnp.bfloat16)
    inverses = lax.all_gather(inverse_low, "shard", axis=0, tiled=True)
    left_terms = jnp.stack(
        [
            jnp.einsum("nc,rc->nr", col_parts[m], inverses[m], preferred_element_type=jnp.float32)
            for m in (0, 4, 6)
        ]
    )
    left = lax.psum(left_terms, "section").astype(jnp.bfloat16)
    right_terms = jnp.stack(
        [
            jnp.einsum("nr,rc->nc", row_parts[m], inverses[m], preferred_element_type=jnp.float32)
            for m in (1, 2, 3, 5, 7)
        ]
    )
    right = lax.psum(right_terms, "tensor").astype(jnp.bfloat16)
    norm_values = norm_terms.astype(jnp.float32)
    router_part = jnp.einsum(
        "en,fn->ef", router_grad, router_grad, preferred_element_type=jnp.float32
    )
    router_sum, norm_total, norm_squares = lax.psum(
        (router_part, jnp.sum(norm_values, axis=1), jnp.sum(norm_values * norm_values, axis=1)),
        "shard",
    )
    router_matrix = (
        factor_decay * old_router_factor
        + (1.0 - factor_decay) * (router_sum / tokens_all)
        + damping * jnp.eye(EXPERTS, dtype=jnp.float32)
    )
    router_inverse = local_inverse(router_matrix)
    router_right = jnp.einsum(
        "en,ef->nf", router_grad, router_inverse, preferred_element_type=jnp.float32
    ).astype(jnp.bfloat16)
    precond_norms = (
        learning_rate
        * norm_total
        / (
            factor_decay * old_norm_diag
            + (1.0 - factor_decay) * (norm_squares / tokens_all)
            + damping
        )
    )
    ids_all = lax.all_gather(token_ids, "shard", axis=0, tiled=True)
    embed_all = lax.all_gather(right[4], "shard", axis=0, tiled=True)
    paired_left = jnp.stack([left[0], left[0], left[0], left[1]])
    attn_terms = jnp.einsum(
        "wnr,wnc->wrc", paired_left, right[:4], preferred_element_type=jnp.float32
    )
    router_term = jnp.einsum("nf,nr->fr", router_right, left[2], preferred_element_type=jnp.float32)
    attn_sum, router_total = lax.psum((attn_terms, router_term), "shard")
    precond_attn = learning_rate * attn_sum
    precond_router = learning_rate * router_total
    vocab_block = VOCAB // n_tensor
    step_rows = math.gcd(vocab_block, 512)
    vocab_start = tensor_rank * vocab_block

    def embed_block(block_index):
        ids_here = vocab_start + block_index * step_rows + lax.iota(jnp.int32, step_rows)
        onehot = (ids_here[:, None] == ids_all[None, :]).astype(jnp.bfloat16)
        summed = jnp.dot(onehot, embed_all, preferred_element_type=jnp.float32)
        tallies = jnp.sum(onehot, axis=1, dtype=jnp.float32)
        return (summed, tallies)

    block_sums, block_counts = lax.map(
        embed_block, jnp.arange(vocab_block // step_rows, dtype=jnp.int32)
    )
    embed_sum = block_sums.reshape(vocab_block, col_block)
    counts = block_counts.reshape(vocab_block)
    divisor = factor_decay * old_embed_diag + (1.0 - factor_decay) * (counts / tokens_all) + damping
    precond_embed = learning_rate * embed_sum / divisor[:, None]
    return (precond_attn, precond_router, precond_norms, precond_embed)


def solution(mesh):
    return jax.shard_map(
        per_device,
        mesh=mesh,
        in_specs=(
            P(None, "shard", ("tensor", "section")),
            P(None, "shard"),
            P("shard"),
            P(None, "shard", ("tensor", "section")),
            P("shard", "tensor", "section"),
            P(),
            P(None, ("tensor", "section")),
            P("tensor"),
        ),
        out_specs=(
            P(None, "tensor", "section"),
            P(None, "tensor"),
            P(None, ("tensor", "section")),
            P("tensor", "section"),
        ),
        check_vma=False,
    )
```

profile of v0, /device:TPU:120, one launch (start us, length us, event | category | flops | bytes accessed | tf_op | source)
XLA Modules:
  0.0 1095.2 jit_solution(1544421095464947552)
XLA Ops:
  8.0 447.8 %while.26 = (s32[]{:T(128)}, bf16[8,256,576]{1,2,0:T(8,128)(2,1)S(1)}, bf16[8,256,288]{1,2,0:T(8,128)(2,1)S(1)}, bf16[8,256,72]{1,2,0:T(8,128)(2,1)}, s32[]{:T(128)}, /*index=5*/s32[]{:T(128)}, s32[]{:T(128)}) while((s32[]{:T(128)}, bf16[8,256,576]{1,2,0:T(8,128)(2,1)S(1)}, bf16[8,256,288]{1,2,0:T(8,128)(2,1)S(1)}, ...), condition=%wide.region_1.2_spmd, body=%wide.region_0.1_spmd.sunk | while | flops 2 | bytes 4608145 | solution.py:64
  8.1 1.4 constant_dynamic-slice_fusion.2
  9.5 53.9 %all-gather.27.cloned.1.call-done = bf16[1,256,2304]{1,2,0:T(8,128)(2,1)} async-done(((bf16[1,256,72]{1,2,0:T(8,128)(2,1)}), bf16[1,256,2304]{1,2,0:T(8,128)(2,1)}) %all-gather.27.cloned.1.call-update) | async-done | bytes 1179664 | tf_op jit(solution)/shard_map/while/body/eval_jaxpr/all_gather | solution.py:59
  63.5 1.0 dynamic-slice_dynamic-update-slice_fusion.4
  64.4 0.9 dynamic-slice_dynamic-update-slice_fusion.5
  65.4 1.4 constant_dynamic-slice_fusion.2
  66.9 52.5 %all-gather.27.cloned.1.call-done = bf16[1,256,2304]{1,2,0:T(8,128)(2,1)} async-done(((bf16[1,256,72]{1,2,0:T(8,128)(2,1)}), bf16[1,256,2304]{1,2,0:T(8,128)(2,1)}) %all-gather.27.cloned.1.call-update) | async-done | bytes 1179664 | tf_op jit(solution)/shard_map/while/body/eval_jaxpr/all_gather | solution.py:59
  119.4 1.0 dynamic-slice_dynamic-update-slice_fusion.4
  121.4 1.4 constant_dynamic-slice_fusion.2
  122.8 52.5 %all-gather.27.cloned.1.call-done = bf16[1,256,2304]{1,2,0:T(8,128)(2,1)} async-done(((bf16[1,256,72]{1,2,0:T(8,128)(2,1)}), bf16[1,256,2304]{1,2,0:T(8,128)(2,1)}) %all-gather.27.cloned.1.call-update) | async-done | bytes 1179664 | tf_op jit(solution)/shard_map/while/body/eval_jaxpr/all_gather | solution.py:59
  175.3 1.0 dynamic-slice_dynamic-update-slice_fusion.4
  177.3 1.4 constant_dynamic-slice_fusion.2
  178.7 52.2 %all-gather.27.cloned.1.call-done = bf16[1,256,2304]{1,2,0:T(8,128)(2,1)} async-done(((bf16[1,256,72]{1,2,0:T(8,128)(2,1)}), bf16[1,256,2304]{1,2,0:T(8,128)(2,1)}) %all-gather.27.cloned.1.call-update) | async-done | bytes 1179664 | tf_op jit(solution)/shard_map/while/body/eval_jaxpr/all_gather | solution.py:59
  230.9 1.0 dynamic-slice_dynamic-update-slice_fusion.4
  232.8 1.4 constant_dynamic-slice_fusion.2
  234.3 52.2 %all-gather.27.cloned.1.call-done = bf16[1,256,2304]{1,2,0:T(8,128)(2,1)} async-done(((bf16[1,256,72]{1,2,0:T(8,128)(2,1)}), bf16[1,256,2304]{1,2,0:T(8,128)(2,1)}) %all-gather.27.cloned.1.call-update) | async-done | bytes 1179664 | tf_op jit(solution)/shard_map/while/body/eval_jaxpr/all_gather | solution.py:59
  286.5 1.0 dynamic-slice_dynamic-update-slice_fusion.4
  288.4 1.4 constant_dynamic-slice_fusion.2
  289.9 52.2 %all-gather.27.cloned.1.call-done = bf16[1,256,2304]{1,2,0:T(8,128)(2,1)} async-done(((bf16[1,256,72]{1,2,0:T(8,128)(2,1)}), bf16[1,256,2304]{1,2,0:T(8,128)(2,1)}) %all-gather.27.cloned.1.call-update) | async-done | bytes 1179664 | tf_op jit(solution)/shard_map/while/body/eval_jaxpr/all_gather | solution.py:59
  342.1 1.0 dynamic-slice_dynamic-update-slice_fusion.4
  344.0 1.4 constant_dynamic-slice_fusion.2
  345.5 52.5 %all-gather.27.cloned.1.call-done = bf16[1,256,2304]{1,2,0:T(8,128)(2,1)} async-done(((bf16[1,256,72]{1,2,0:T(8,128)(2,1)}), bf16[1,256,2304]{1,2,0:T(8,128)(2,1)}) %all-gather.27.cloned.1.call-update) | async-done | bytes 1179664 | tf_op jit(solution)/shard_map/while/body/eval_jaxpr/all_gather | solution.py:59
  398.0 1.0 dynamic-slice_dynamic-update-slice_fusion.4
  399.9 1.4 constant_dynamic-slice_fusion.2
  401.4 52.5 %all-gather.27.cloned.1.call-done = bf16[1,256,2304]{1,2,0:T(8,128)(2,1)} async-done(((bf16[1,256,72]{1,2,0:T(8,128)(2,1)}), bf16[1,256,2304]{1,2,0:T(8,128)(2,1)}) %all-gather.27.cloned.1.call-update) | async-done | bytes 1179664 | tf_op jit(solution)/shard_map/while/body/eval_jaxpr/all_gather | solution.py:59
  453.9 1.0 dynamic-slice_dynamic-update-slice_fusion.4
  455.9 3.7 fusion.83
  459.7 70.8 %reduce-scatter.2.cloned.1.call-done = f32[1,576,288]{1,2,0:T(8,128)} async-done(((f32[8,576,288]{1,2,0:T(8,128)}), f32[1,576,288]{1,2,0:T(8,128)}) %reduce-scatter.2.cloned.1.call-update) | async-done | bytes 663568 | tf_op jit(solution)/shard_map/reduce_scatter | solution.py:68
  530.4 2.1 fusion.48
  532.5 67.2 %psum.56 = f32[1]{0:T(128)} all-reduce(f32[1]{0:T(128)} %bitcast.4), channel_id=1, replica_groups=mesh['shard'=8,'tensor'=4,'section'=8] {'tensor','section'}, use_global_device_ids=true, to_apply=%region_4.5 | all-reduce | flops 1 | bytes 8 | tf_op jit(solution)/shard_map/psum | solution.py:74
  600.6 1.9 copy.32
  603.2 76.2 %all-gather.19.cloned.1.call-done = bf16[1,2304,288]{2,0,1:T(2,128)(2,1)} async-done(((bf16[1,576,288]{2,0,1:T(2,128)(2,1)}), bf16[1,2304,288]{2,0,1:T(2,128)(2,1)}) %all-gather.19.cloned.1.call-update) | async-done | bytes 1327120 | tf_op jit(solution)/shard_map/all_gather | solution.py:81
  679.4 8.4 copy.33
  687.8 21.7 %all-gather.17.cloned.1.call-done = bf16[1,576,2304]{1,2,0:T(8,128)(2,1)} async-done(((bf16[1,576,288]{1,2,0:T(8,128)(2,1)}), bf16[1,576,2304]{1,2,0:T(8,128)(2,1)}) %all-gather.17.cloned.1.call-update) | async-done | bytes 2654224 | tf_op jit(solution)/shard_map/all_gather | solution.py:82
  709.6 3.8 fusion.29
  714.2 38.9 %all-gather.25.cloned.1.call-done = bf16[4,576,288]{1,2,0:T(8,128)(2,1)} async-done(((bf16[1,576,288]{1,2,0:T(8,128)(2,1)}), bf16[4,576,288]{1,2,0:T(8,128)(2,1)}) %all-gather.25.cloned.1.call-update) | async-done | bytes 1327120 | tf_op jit(solution)/shard_map/all_gather | solution.py:83
  753.1 2.1 copy.34
  755.3 2.0 reshape.184
  757.3 27.5 %all-gather.15.cloned.1.call-done = bf16[1,576,2304]{1,2,0:T(8,128)(2,1)} async-done(((bf16[1,576,288]{1,2,0:T(8,128)(2,1)}), bf16[1,576,2304]{1,2,0:T(8,128)(2,1)}) %all-gather.15.cloned.1.call-update) | async-done | bytes 2654224 | tf_op jit(solution)/shard_map/all_gather | solution.py:84
  784.8 4.2 fusion.21
  789.2 18.6 %psum.60 = f32[8,8]{1,0:T(8,128)S(1)} all-reduce(f32[8,8]{1,0:T(8,128)S(1)} %fusion.84), channel_id=1, replica_groups=mesh['shard'=8,'tensor'=4,'section'=8] {'shard'}, use_global_device_ids=true, to_apply=%region_8.9 | all-reduce | flops 64 | bytes 512 | tf_op jit(solution)/shard_map/psum | solution.py:105
  809.8 15.1 %all-gather.4 = s32[8,1,256]{2,1,0:T(1,128)S(1)} all-gather(s32[1,1,256]{2,1,0:T(1,128)S(1)} %bitcast.152), channel_id=1, replica_groups=mesh['shard'=8,'tensor'=4,'section'=8] {'shard'}, dimensions={0}, use_global_device_ids=true | all-gather | bytes 9216 | tf_op jit(solution)/shard_map/all_gather | solution.py:127
  825.3 10.1 all-gather.21.cloned.1.call-done
  835.4 2.0 fusion.44
  837.4 2.0 fusion.43
  839.4 2.0 fusion.42
  841.3 2.0 fusion.41
  843.3 2.0 fusion.40
  845.3 54.0 %all-reduce.6 = bf16[5,256,288]{1,2,0:T(8,128)(2,1)S(1)} all-reduce(f32[5,256,288]{1,2,0:T(8,128)} %fusion.40), channel_id=1, replica_groups=mesh['shard'=8,'tensor'=4,'section'=8] {'tensor'}, use_global_device_ids=true, to_apply=%region_6.7 | all-reduce | flops 368640 | bytes 2211840 | tf_op jit(solution)/shard_map/psum | solution.py:100
  900.1 1.4 convolution_bitcast_fusion.2
  901.5 1.4 convolution_bitcast_fusion.1
  903.0 1.4 convolution_bitcast_fusion
  904.5 48.6 %all-reduce.7 = bf16[3,256,576]{1,2,0:T(8,128)(2,1)S(1)} all-reduce(f32[3,256,576]{1,2,0:T(8,128)S(1)} %pad_maximum_fusion), channel_id=1, replica_groups=mesh['shard'=8,'tensor'=4,'section'=8] {'section'}, use_global_device_ids=true, to_apply=%region_5.6 | all-reduce | flops 442368 | bytes 2654208 | tf_op jit(solution)/shard_map/psum | solution.py:93
  953.4 36.5 %all-reduce = (f32[8,576]{1,0:T(8,128)S(1)}, f32[2,72]{1,0:T(2,128)S(1)}, f32[2,72]{1,0:T(2,128)S(1)}) all-reduce(f32[8,576]{1,0:T(8,128)S(1)} %fusion.45, f32[2,72]{1,0:T(2,128)S(1)} %get-tuple-element.173, f32[2,72]{1,0:T(2,128)S(1)} %get-tuple-element.172), channel_id=1, replica_groups=mesh['shard'=8,'tensor'=4,'section'=8] {'shard'}, use_global_device_ids=true, to_apply=%region_10.11 | all-reduce | flops 4896 | bytes 39168 | tf_op jit(solution)/shard_map/psum | solution.py:134
  990.5 2.3 fusion.34
  994.0 2.5 copy.35
  996.6 17.2 %while.27 = (s32[]{:T(128)}, f32[4,512,288]{1,2,0:T(8,128)S(1)}, f32[4,512]{1,0:T(4,128)S(1)}, s32[4]{0:T(128)S(1)}, s32[]{:T(128)}, /*index=5*/s32[2048]{0:T(10...) while((s32[]{:T(128)}, f32[4,512,288]{1,2,0:T(8,128)S(1)}, f32[4,512]{1,0:T(4,128)S(1)}, ...), condition=%wide.region_17.18_spmd, body=%wide.region_15.17_spmd.sunk | while | flops 609222656 | bytes 1798293 | solution.py:148
  997.7 2.5 fusion.99
  1001.9 2.7 fusion.99
  1006.4 2.5 fusion.99
  1010.7 2.5 fusion.99
  1014.8 1.7 broadcast_divide_fusion
  1016.5 67.6 %all-reduce.5.cloned.1.call-done = f32[4,576,288]{1,2,0:T(8,128)} async-done(((f32[4,576,288]{1,2,0:T(8,128)}), f32[4,576,288]{1,2,0:T(8,128)}) %all-reduce.5.cloned.1.call-update) | async-done | bytes 2654224 | tf_op jit(solution)/shard_map/psum | solution.py:134
  1084.1 3.7 broadcast_multiply_fusion
  (111 shorter events, 19.1 us)
Async XLA Ops:
  8.0 781.1 %copy-start = (bf16[8,256]{1,0:T(8,128)(2,1)S(1)}, bf16[8,256]{1,0:T(8,128)(2,1)}, u32[]{:S(2)}) copy-start(bf16[8,256]{1,0:T(8,128)(2,1)} %param.13) | copy-start | bytes 12292
  8.1 55.4 %all-gather.27.cloned.1.call-start = ((), (), s32[]{:S(2)}) async-start(), calls=%async_computation.9 | async-start | bytes 1216512 | tf_op jit(solution)/shard_map/while/body/eval_jaxpr/all_gather | solution.py:59
  65.4 54.0 %all-gather.27.cloned.1.call-start = ((), (), s32[]{:S(2)}) async-start(), calls=%async_computation.9 | async-start | bytes 1216512 | tf_op jit(solution)/shard_map/while/body/eval_jaxpr/all_gather | solution.py:59
  121.3 54.0 %all-gather.27.cloned.1.call-start = ((), (), s32[]{:S(2)}) async-start(), calls=%async_computation.9 | async-start | bytes 1216512 | tf_op jit(solution)/shard_map/while/body/eval_jaxpr/all_gather | solution.py:59
  177.2 53.7 %all-gather.27.cloned.1.call-start = ((), (), s32[]{:S(2)}) async-start(), calls=%async_computation.9 | async-start | bytes 1216512 | tf_op jit(solution)/shard_map/while/body/eval_jaxpr/all_gather | solution.py:59
  232.8 53.7 %all-gather.27.cloned.1.call-start = ((), (), s32[]{:S(2)}) async-start(), calls=%async_computation.9 | async-start | bytes 1216512 | tf_op jit(solution)/shard_map/while/body/eval_jaxpr/all_gather | solution.py:59
  288.4 53.7 %all-gather.27.cloned.1.call-start = ((), (), s32[]{:S(2)}) async-start(), calls=%async_computation.9 | async-start | bytes 1216512 | tf_op jit(solution)/shard_map/while/body/eval_jaxpr/all_gather | solution.py:59
  344.0 54.0 %all-gather.27.cloned.1.call-start = ((), (), s32[]{:S(2)}) async-start(), calls=%async_computation.9 | async-start | bytes 1216512 | tf_op jit(solution)/shard_map/while/body/eval_jaxpr/all_gather | solution.py:59
  399.9 54.0 %all-gather.27.cloned.1.call-start = ((), (), s32[]{:S(2)}) async-start(), calls=%async_computation.9 | async-start | bytes 1216512 | tf_op jit(solution)/shard_map/while/body/eval_jaxpr/all_gather | solution.py:59
  455.8 3.7 copy-start.5
  455.8 3.7 copy-start.7
  455.8 74.6 %reduce-scatter.2.cloned.1.call-start = ((), (), s32[]{:S(2)}) async-start(), calls=%async_computation.1 | async-start | bytes 6635520 | tf_op jit(solution)/shard_map/reduce_scatter | solution.py:68
  459.5 70.9 %copy-start.8 = (f32[1,576,288]{1,2,0:T(8,128)S(1)}, f32[1,576,288]{1,2,0:T(8,128)}, u32[]{:S(2)}) copy-start(f32[1,576,288]{1,2,0:T(8,128)} %param.16) | copy-start | bytes 1990660
  459.6 219.8 %all-gather.19.cloned.1.call-start = ((), (), s32[]{:S(2)}) async-start(), calls=%async_computation.4 | async-start | bytes 4423680 | tf_op jit(solution)/shard_map/all_gather | solution.py:81
  532.5 70.1 %copy-start.1 = (bf16[1,576,288]{1,2,0:T(8,128)(2,1)}, bf16[1,576,288]{1,2,0:T(8,128)(2,1)S(1)}, u32[]{:S(2)}) copy-start(bf16[1,576,288]{1,2,0:T(8,128)(2,1)S(1)} %get-tuple-element.206) | copy-start | bytes 995332
  600.6 87.2 %copy-start.3 = (bf16[1,576,288]{1,2,0:T(8,128)(2,1)}, bf16[1,576,288]{1,2,0:T(8,128)(2,1)S(1)}, u32[]{:S(2)}) copy-start(bf16[1,576,288]{1,2,0:T(8,128)(2,1)S(1)} %fusion.50) | copy-start | bytes 995332
  602.6 107.0 %all-gather.17.cloned.1.call-start = ((), (), s32[]{:S(2)}) async-start(), calls=%async_computation.3 | async-start | bytes 3317760 | tf_op jit(solution)/shard_map/all_gather | solution.py:82
  603.2 149.9 %all-gather.25.cloned.1.call-start = ((), (), s32[]{:S(2)}) async-start(), calls=%async_computation.8 | async-start | bytes 1843200 | tf_op jit(solution)/shard_map/all_gather | solution.py:83
  713.4 71.4 %all-gather.15.cloned.1.call-start = ((), (), s32[]{:S(2)}) async-start(), calls=%async_computation.2 | async-start | bytes 3317760 | tf_op jit(solution)/shard_map/all_gather | solution.py:84
  714.1 70.7 %copy-start.2 = (bf16[1,576,288]{1,2,0:T(8,128)(2,1)S(1)}, bf16[1,576,288]{1,2,0:T(8,128)(2,1)}, u32[]{:S(2)}) copy-start(bf16[1,576,288]{1,2,0:T(8,128)(2,1)} %copy-done.1) | copy-start | bytes 995332
  714.1 121.2 %all-gather.21.cloned.1.call-start = ((), (), s32[]{:S(2)}) async-start(), calls=%async_computation.5 | async-start | bytes 3317760 | tf_op jit(solution)/shard_map/all_gather | solution.py:86
  757.3 50.6 %copy-start.11 = (f32[8,8]{1,0:T(8,128)S(1)}, f32[8,8]{1,0:T(8,128)}, u32[]{:S(2)}) copy-start(f32[8,8]{1,0:T(8,128)} %param.17) | copy-start | bytes 772
  757.3 52.5 %copy-start.12 = (s32[256]{0:T(256)S(1)}, s32[256]{0:T(256)}, u32[]{:S(2)}) copy-start(s32[256]{0:T(256)} %param.14) | copy-start | bytes 3076
  757.3 67.7 %copy-start.9 = (bf16[2,256,72]{1,2,0:T(8,128)(2,1)S(1)}, bf16[2,256,72]{1,2,0:T(8,128)(2,1)}, u32[]{:S(2)}) copy-start(bf16[2,256,72]{1,2,0:T(8,128)(2,1)} %param.15) | copy-start | bytes 221188
  757.3 78.1 %copy-start.6 = (bf16[8,256,576]{1,2,0:T(8,128)(2,1)S(1)}, bf16[8,256,576]{1,2,0:T(8,128)(2,1)}, u32[]{:S(2)}) copy-start(bf16[8,256,576]{1,2,0:T(8,128)(2,1)} %copy-done.5) | copy-start | bytes 7077892
  789.0 205.0 %all-gather.23.cloned.1.call-start = ((), (), s32[]{:S(2)}) async-start(), calls=%async_computation.7 | async-start | bytes 1327104 | tf_op jit(solution)/shard_map/all_gather | solution.py:128
  900.0 184.1 %all-reduce.5.cloned.1.call-start = ((), (), s32[]{:S(2)}) async-start(), calls=%async_computation.6 | async-start | bytes 5898240 | tf_op jit(solution)/shard_map/psum | solution.py:134
  992.8 0.7 copy-start.13
  992.8 3.8 copy-start.4
  1014.1 0.7 copy-start.10
Sparse Core Ops, SparseCore 0:
  12.1 51.3 all-gather.26
  69.4 49.8 all-gather.26
  125.3 49.8 all-gather.26
  180.9 49.8 all-gather.26
  236.5 49.8 all-gather.26
  292.1 49.8 all-gather.26
  348.0 49.8 all-gather.26
  403.9 49.8 all-gather.26
Sparse Core Ops, SparseCore 1:
  459.7 70.7 reduce-scatter.1
  602.7 76.7 all-gather.18
  681.3 28.3 all-gather.16
  713.5 39.6 all-gather.24
  755.1 29.6 all-gather.14
  789.1 46.2 all-gather.20
  900.1 43.5 all-gather.22
  992.9 91.2 all-reduce.4
where the time goes:
time: 1100 us
  waiting for transfers between devices  735 us (67%)
  blocking collectives  240 us (22%)
  local copies, waits for them, and re-layouts  48.6 us (4%)
  matrix products  39 us (4%)
  between operations  17.2 us (2%)
  other arithmetic  12.2 us (1%)
    all_gather x8, waiting for transfers between devices, collect(): whole = lax.all_gather(piece, ('tensor', 'section'), axis=1, tiled=True)  421 us
    all_gather x1, waiting for transfers between devices, per_device(): first_cols = lax.all_gather(first_low, 'tensor', axis=1, tiled=True)  76.2 us
    reduce_scatter x1, waiting for transfers between devices, per_device(): lax.psum_scatter(partial_value, 'shard', scatter_dimension=0, tiled=True)  70.8 us
    psum x1, waiting for transfers between devices, per_device(): attn_sum, router_total = lax.psum((attn_terms, router_term), 'shard')  67.6 us
    psum x1, blocking collectives, per_device(): trace = lax.psum(diag_part, ('tensor', 'section'))  67.2 us
    psum x1, blocking collectives, per_device(): right = lax.psum(right_terms, 'tensor').astype(jnp.bfloat16)  54 us
    psum x1, blocking collectives, per_device(): left = lax.psum(left_terms, 'section').astype(jnp.bfloat16)  48.6 us
    all_gather x1, waiting for transfers between devices, per_device(): lax.all_gather(image.astype(jnp.bfloat16), 'tensor', axis=1, tiled=True)  38.9 us
  transfers between devices with their start and end apart: 16, of which 15 were waited for; matrix products, arithmetic and copies ran while one was open for 4% of the time, Pallas kernels for 0%

commit v1 on v0

v1 whole, which is shorter than its diff:
```python
import jax
import jax.numpy as jnp
from jax import lax
from jax.experimental import pallas as pl
from jax.experimental.pallas import tpu as pltpu
from jax.sharding import PartitionSpec as P

D = 2304
TOKENS = 2048
FEAT = 72
TOK = 256
WIDE = 576
HALF = 288
EXPERTS = 8
RATE = 0.05
RUN = 144
NT = (((1,), (1,)), ((), ()))
BF = jnp.bfloat16
F32 = jnp.float32


def here():
    s = lax.axis_index("shard")
    t = lax.axis_index("tensor")
    c = lax.axis_index("section")
    x, zl, y, k = lax.rem(s, 4), lax.div(s, 4), lax.div(c, 2), lax.rem(c, 2)
    return x, y, 2 * t + zl, k, zl, t


def at(x, y, z, k):
    return (lax.rem(z, 2) * 4 + x, lax.div(z, 2), 2 * y + k)


def step(v, d, n):
    return lax.rem(v + d, n)


def copy_to(src, dst, send, recv, device):
    return pltpu.make_async_remote_copy(
        src_ref=src,
        dst_ref=dst,
        send_sem=send,
        recv_sem=recv,
        device_id=device,
        device_id_type=pl.DeviceIdType.MESH,
    )


def signal(sem, device):
    pl.semaphore_signal(sem, inc=1, device_id=device, device_id_type=pl.DeviceIdType.MESH)


def precondition_kernel(
    feats, old, router_grad, ids, norm_terms, old_router, old_norm,
    out, rights, all_ids, norms,
    small, small_all,
    AT, OB, PM, PS, PR, MB, UB, UF, TR,
    z_send, z_recv, o_send, o_recv, ox_send, ox_recv, od_send, od_recv,
    p_send, p_recv, px_send, px_recv, u_send, u_recv, t_send, t_recv, s_send, s_recv,
):
    x, y, z, k, zl, t = here()
    s = zl * 4 + x
    me = at(x, y, z, k)
    xp, xm, xo = step(x, 1, 4), step(x, 3, 4), step(x, 2, 4)
    yp, ym, yo = step(y, 1, 4), step(y, 3, 4), step(y, 2, 4)
    east, west = at(xp, y, z, k), at(xm, y, z, k)
    north, south = at(x, yp, z, k), at(x, ym, z, k)
    partner = at(x, y, z, 1 - k)
    old_to = at(t, y, s, k)
    old_from = (z, x, 2 * y + k)
    old_stays = jnp.logical_and(x == t, z == s)

    barrier = pltpu.get_barrier_semaphore()
    for d in range(8):
        zz = step(z, d, 8)
        if d:
            signal(barrier, at(x, y, zz, k))
        signal(barrier, at(x, y, zz, 1 - k))
    for device in (east, west, north, south, at(x, yo, z, k)):
        signal(barrier, device)
    for d in range(1, 8):
        signal(barrier, (step(s, d, 8), t, 2 * y + k))

    @pl.when(jnp.logical_not(old_stays))
    def _():
        signal(barrier, old_to)
        signal(barrier, old_from)

    @pl.when(old_stays)
    def _():
        signal(barrier, partner)
        signal(barrier, partner)

    pl.semaphore_wait(barrier, 15 + 5 + 7 + 2)

    waits = []

    def rows_of(tt, yy, kk):
        return pl.ds(pl.multiple_of(tt * WIDE + yy * RUN + kk * FEAT, 8), FEAT)

    for d in range(8):
        zz = step(z, d, 8)
        src = feats.at[zz]
        dst = AT.at[x, rows_of(t, y, k), :]
        rsem = z_recv.at[2 * t + k]
        if d:
            cp = copy_to(src, dst, z_send.at[d], rsem, at(x, y, zz, zl))
            cp.start()
            waits.append(cp)
        else:

            @pl.when(k == zl)
            def _():
                pltpu.make_async_copy(src, dst, rsem).start()

            @pl.when(k != zl)
            def _():
                copy_to(src, dst, z_send.at[0], rsem, partner).start()

    old_dst = OB.at[t, pl.ds(pl.multiple_of(k * HALF, 16), HALF), :]

    @pl.when(old_stays)
    def _():
        pltpu.make_async_copy(old, old_dst, o_recv.at[0]).start()

    @pl.when(jnp.logical_not(old_stays))
    def _():
        copy_to(old, old_dst, o_send.at[0], o_recv.at[0], old_to).start()

    small[0:8, :] = router_grad[...].astype(F32)
    small[8:16, :] = jnp.broadcast_to(ids[...].astype(F32), (8, TOK))
    for i in range(2):
        terms = norm_terms[i].astype(F32)
        small[16 + i : 17 + i, 0:FEAT] = jnp.sum(terms, axis=0, keepdims=True)
        small[18 + i : 19 + i, 0:FEAT] = jnp.sum(terms * terms, axis=0, keepdims=True)
    for d in range(1, 8):
        cp = copy_to(small, small_all.at[s], s_send.at[d - 1], s_recv.at[s], (step(s, d, 8), t, 2 * y + k))
        cp.start()
        waits.append(cp)
    own_small = pltpu.make_async_copy(small, small_all.at[s], s_recv.at[s])
    own_small.start()

    def chunk(xx, yy, tt):
        return AT.at[xx, pl.ds(pl.multiple_of(tt * WIDE + yy * RUN, 16), RUN), :]

    n_sent = [0]

    def pass_on(xx, yy, tt, device):
        ref = chunk(xx, yy, tt)
        cp = copy_to(ref, ref, p_send.at[n_sent[0]], p_recv.at[xx * 16 + yy * 4 + tt], device)
        n_sent[0] += 1
        cp.start()
        waits.append(cp)

    def arrive(xx, yy, tt):
        ref = chunk(xx, yy, tt)
        copy_to(ref, ref, p_send.at[0], p_recv.at[xx * 16 + yy * 4 + tt], partner).wait_recv()

    for tt in range(4):
        for kk in range(2):
            ref = AT.at[x, rows_of(tt, y, kk), :]
            copy_to(ref, ref, z_send.at[0], z_recv.at[2 * tt + kk], partner).wait_recv()
        for device in (north, south, east, west) if tt < 2 else (east, west, north, south):
            pass_on(x, y, tt, device)

    def old_part(tt, kk, hh):
        start = kk * HALF + hh * RUN
        return OB.at[tt, pl.ds(pl.multiple_of(start, 16), RUN), :]

    def old_block(tt, kk):
        return OB.at[tt, pl.ds(pl.multiple_of(kk * HALF, 16), HALF), :]

    m_sent = [0]

    def old_on(tt, hh, device):
        ref = old_part(tt, k, hh)
        cp = copy_to(ref, ref, ox_send.at[m_sent[0]], ox_recv.at[2 * tt + hh], device)
        m_sent[0] += 1
        cp.start()
        waits.append(cp)

    def old_arrive(tt, hh):
        ref = old_part(tt, k, hh)
        copy_to(ref, ref, ox_send.at[0], ox_recv.at[2 * tt + hh], partner).wait_recv()

    def old_over(i, tt):
        ref = old_block(tt, k)
        cp = copy_to(ref, ref, od_send.at[i], od_recv.at[tt], partner)
        cp.start()
        waits.append(cp)

    pltpu.make_async_copy(old_block(x, k), old_block(x, k), o_recv.at[0]).wait()
    for hh in range(2):
        old_on(x, hh, east)
        old_on(x, hh, west)
    old_over(0, x)

    for tt in range(2):
        arrive(x, ym, tt)
        if tt == 0:
            pass_on(x, ym, tt, north)
        pass_on(x, ym, tt, east)
        pass_on(x, ym, tt, west)
        arrive(xm, y, 2 + tt)
        if tt == 0:
            pass_on(xm, y, 2, east)
        pass_on(xm, y, 2 + tt, north)
        pass_on(xm, y, 2 + tt, south)
    for tt in (1, 0):
        arrive(x, yp, tt)
        if tt == 1:
            pass_on(x, yp, tt, south)
        pass_on(x, yp, tt, east)
        pass_on(x, yp, tt, west)
        arrive(xp, y, 2 + tt)
        if tt == 1:
            pass_on(xp, y, 3, west)
        pass_on(xp, y, 2 + tt, north)
        pass_on(xp, y, 2 + tt, south)
    arrive(xm, y, 0)
    pass_on(xm, y, 0, east)
    arrive(xp, y, 1)
    pass_on(xp, y, 1, west)
    arrive(x, ym, 2)
    pass_on(x, ym, 2, north)
    arrive(x, yp, 3)
    pass_on(x, yp, 3, south)
    for tt in range(2):
        arrive(x, yo, tt)
        pass_on(x, yo, tt, east)
        pass_on(x, yo, tt, west)
        arrive(xo, y, 2 + tt)
        pass_on(xo, y, 2 + tt, north)
        pass_on(xo, y, 2 + tt, south)
    for hh in range(2):
        old_arrive(xm, hh)
        if hh == 0:
            old_on(xm, 0, east)
    old_over(1, xm)
    for hh in (1, 0):
        old_arrive(xp, hh)
        if hh == 1:
            old_on(xp, 1, west)
    old_over(2, xp)
    for aa in (1, 3, 2):
        yy, xx = step(y, aa, 4), step(x, aa, 4)
        arrive(xm, yy, 0)
        pass_on(xm, yy, 0, east)
        arrive(xp, yy, 1)
        pass_on(xp, yy, 1, west)
        arrive(xx, ym, 2)
        pass_on(xx, ym, 2, north)
        arrive(xx, yp, 3)
        pass_on(xx, yp, 3, south)
    for aa in range(4):
        yy, xx = step(y, aa, 4), step(x, aa, 4)
        arrive(xm, yy, 1)
        arrive(xp, yy, 0)
        arrive(xx, ym, 3)
        arrive(xx, yp, 2)
        arrive(xo, yy, 0)
        arrive(xo, yy, 1)
        arrive(xx, yo, 2)
        arrive(xx, yo, 3)
    for hh in range(2):
        old_arrive(xo, hh)
    old_over(3, xo)

    my_rows = pl.ds(pl.multiple_of(y * WIDE, 16), WIDE)

    @pl.loop(0, 4)
    def _(tt):
        block = pl.ds(pl.multiple_of(tt * WIDE, 16), WIDE)
        total = jnp.zeros((WIDE, WIDE), F32)
        for xx in range(4):
            total += lax.dot_general(AT[xx, my_rows, :], AT[xx, block, :], NT, preferred_element_type=F32)
        PM[tt] = total
        PS[tt] = total.astype(BF)
        copy_to(PS.at[tt], PR.at[tt], px_send.at[tt], px_recv.at[tt], partner).start()

    for aa in range(4):
        ref = old_block(step(x, aa, 4), 1 - k)
        copy_to(ref, ref, od_send.at[0], od_recv.at[step(x, aa, 4)], partner).wait_recv()

    TR[y] = jnp.zeros((8, 128), F32)
    row = lax.broadcasted_iota(jnp.int32, (WIDE, WIDE), 0) + y * WIDE
    col = lax.broadcasted_iota(jnp.int32, (WIDE, WIDE), 1)

    @pl.loop(0, 4)
    def _(tt):
        copy_to(PS.at[tt], PR.at[tt], px_send.at[tt], px_recv.at[tt], partner).wait()
        fresh = PM[tt] + PR[tt].astype(F32)
        eye = (row == col + tt * WIDE).astype(F32)
        matrix = 0.5 * OB[tt].astype(F32) + (0.5 / TOKENS) * fresh + 0.01 * eye
        TR[y] += jnp.full((8, 128), jnp.sum(matrix * eye), F32)
        MB[tt] = matrix.astype(BF)

    for i, dd in enumerate((1, 3, 2)):
        cp = copy_to(TR.at[y], TR.at[y], t_send.at[i], t_recv.at[y], at(x, step(y, dd, 4), z, k))
        cp.start()
        waits.append(cp)

    def times_matrix(block_of):
        total = jnp.zeros((WIDE, TOK), F32)
        for tt in range(4):
            total += jnp.dot(MB[tt], block_of(tt), preferred_element_type=F32)
        return total

    def spread(r):
        def part(yy, hh):
            return UB.at[r, yy, pl.ds(hh * HALF, HALF), :]

        def put(i, yy, hh, device):
            ref = part(yy, hh)
            cp = copy_to(ref, ref, u_send.at[6 * r + i], u_recv.at[8 * r + 2 * yy + hh], device)
            cp.start()
            waits.append(cp)

        def got(yy, hh):
            ref = part(yy, hh)
            copy_to(ref, ref, u_send.at[0], u_recv.at[8 * r + 2 * yy + hh], partner).wait_recv()

        put(0, y, 0, north)
        put(1, y, 1, south)
        put(2, y, 1, north)
        put(3, y, 0, south)
        got(ym, 0)
        put(4, ym, 0, north)
        got(yp, 1)
        put(5, yp, 1, south)
        got(ym, 1)
        got(yp, 0)
        got(yo, 0)
        got(yo, 1)

    u = times_matrix(lambda tt: AT[x, pl.ds(tt * WIDE, WIDE), :])
    UF[0] = u
    UB[0, y] = u.astype(BF)
    spread(0)
    u = times_matrix(lambda tt: UB[0, tt])
    UF[1] = u
    UB[1, y] = u.astype(BF)
    spread(1)
    u = times_matrix(lambda tt: UB[1, tt])
    for dd in range(1, 4):
        yy = step(y, dd, 4)
        copy_to(TR.at[yy], TR.at[yy], t_send.at[0], t_recv.at[yy], partner).wait_recv()
    trace = (TR[0] + TR[1] + TR[2] + TR[3])[0:1, 0:1]
    scale = D / (3.0 * trace)
    first = AT[x, my_rows, :].astype(F32)
    out[...] = (
        scale * (4.0 * first - scale * (6.0 * UF[0] - scale * (4.0 * UF[1] - scale * u)))
    ).astype(BF)

    for cp in waits:
        cp.wait_send()

    @pl.when(k != zl)
    def _():
        copy_to(feats.at[z], feats.at[z], z_send.at[0], z_recv.at[0], partner).wait_send()

    @pl.when(jnp.logical_not(old_stays))
    def _():
        copy_to(old, old_block(0, 0), o_send.at[0], o_recv.at[0], partner).wait_send()

    for d in range(8):
        ss = step(s, d, 8)
        copy_to(small, small_all.at[ss], s_send.at[0], s_recv.at[ss], partner).wait_recv()

    sums = jnp.zeros((EXPERTS, EXPERTS), F32)
    stats = jnp.zeros((8, TOK), F32)
    for ss in range(8):
        grad = small_all[ss, 0:8, :].astype(BF)
        sums += lax.dot_general(grad, grad, NT, preferred_element_type=F32)
        stats += small_all[ss, 16:24, :]
        all_ids[ss : ss + 1, :] = small_all[ss, 8:9, :]
    norms[...] = RATE * stats[0:2, 0:FEAT] / (
        0.5 * old_norm[...] + (0.5 / TOKENS) * stats[2:4, 0:FEAT] + 0.01
    )
    eye8 = (
        lax.broadcasted_iota(jnp.int32, (8, 8), 0) == lax.broadcasted_iota(jnp.int32, (8, 8), 1)
    ).astype(F32)
    matrix8 = 0.5 * old_router[...] + (0.5 / TOKENS) * sums + 0.01 * eye8
    scale8 = EXPERTS / (3.0 * jnp.sum(jnp.sum(matrix8 * eye8, axis=1, keepdims=True), axis=0, keepdims=True))
    low8 = matrix8.astype(BF)
    first8 = 2.0 * scale8 * eye8 - scale8 * scale8 * low8.astype(F32)
    image8 = jnp.dot(low8, first8.astype(BF), preferred_element_type=F32).astype(BF)
    inverse8 = (
        2.0 * first8 - jnp.dot(first8.astype(BF), image8, preferred_element_type=F32)
    ).astype(BF)
    mine = small_all[k * 4 + x, 0:8, :].astype(BF)
    rights[...] = lax.dot_general(
        inverse8, mine, (((0,), (0,)), ((), ())), preferred_element_type=F32
    ).astype(BF)


DMA = pltpu.SemaphoreType.DMA
VM = pl.BlockSpec(memory_space=pltpu.VMEM)


def precondition(*operands):
    return pl.pallas_call(
        precondition_kernel,
        out_shape=(
            jax.ShapeDtypeStruct((WIDE, TOK), BF),
            jax.ShapeDtypeStruct((8, TOK), BF),
            jax.ShapeDtypeStruct((8, TOK), F32),
            jax.ShapeDtypeStruct((2, FEAT), F32),
        ),
        in_specs=[VM] * 7,
        out_specs=[VM] * 4,
        scratch_shapes=[
            pltpu.VMEM((24, TOK), F32),
            pltpu.VMEM((8, 24, TOK), F32),
            pltpu.VMEM((4, D, TOK), BF),
            pltpu.VMEM((4, WIDE, WIDE), BF),
            pltpu.VMEM((4, WIDE, WIDE), F32),
            pltpu.VMEM((4, WIDE, WIDE), BF),
            pltpu.VMEM((4, WIDE, WIDE), BF),
            pltpu.VMEM((4, WIDE, WIDE), BF),
            pltpu.VMEM((2, 4, WIDE, TOK), BF),
            pltpu.VMEM((2, WIDE, TOK), F32),
            pltpu.VMEM((4, 8, 128), F32),
        ]
        + [DMA((n,)) for n in (8, 8, 1, 1, 6, 8, 4, 4, 60, 64, 4, 4, 12, 16, 3, 4, 7, 8)],
        compiler_params=pltpu.CompilerParams(
            collective_id=0, has_side_effects=True, vmem_limit_bytes=60 * 1024 * 1024
        ),
    )(*operands)


def combine_kernel(
    lt, rights,
    AO, EB, router,
    LB, RB, RX, PB, QB, SB, RSF, RSB, RP,
    l_send, l_recv, r_send, r_recv, b_send, c_send, c_recv, d_send, d_recv, q_send, q_recv,
    g_send, g_recv, e_send, e_recv, v_send, v_recv, n_send, n_recv, w_send, w_recv,
):
    x, y, z, k, zl, t = here()
    me = at(x, y, z, k)
    xp, xm, xo = step(x, 1, 4), step(x, 3, 4), step(x, 2, 4)
    yp, ym = step(y, 1, 4), step(y, 3, 4)
    east, west = at(xp, y, z, k), at(xm, y, z, k)
    north, south = at(x, yp, z, k), at(x, ym, z, k)
    partner = at(x, y, z, 1 - k)
    pair = at(x, y, 2 * t + 1 - zl, k)

    barrier = pltpu.get_barrier_semaphore()
    for dy in range(4):
        for dz in range(8):
            if dy or dz:
                signal(barrier, at(x, step(y, dy, 4), step(z, dz, 8), k))
    for dx in range(4):
        for kk in range(2):
            if dx or kk:
                signal(barrier, at(step(x, dx, 4), y, z, lax.rem(k + kk, 2)))
    pl.semaphore_wait(barrier, 31 + 7)

    pending = []

    def send(make, cond=None):
        if cond is None:
            make().start()
        else:

            @pl.when(cond)
            def _():
                make().start()

        pending.append((cond, make))

    def local(src, dst, sem, cond):
        @pl.when(cond)
        def _():
            pltpu.make_async_copy(src, dst, sem).start()

    def half(ref, hh, rows=HALF):
        return ref.at[pl.ds(hh * rows, rows), :]

    for i, (p, zz) in enumerate(((0, 0), (0, 1), (1, 1))):
        for hh in range(2):
            src, dst, rsem = half(lt, hh), half(LB.at[p], hh), l_recv.at[2 * p + hh]
            target = at(x, y, 2 * y + zz, k)
            cond = z == 4 * p
            if (p, zz) == (0, 0):
                local(src, dst, rsem, jnp.logical_and(cond, y == 0))
                cond = jnp.logical_and(cond, y != 0)
            send(
                lambda src=src, dst=dst, i=i, hh=hh, rsem=rsem, target=target: copy_to(
                    src, dst, l_send.at[2 * i + hh], rsem, target
                ),
                cond,
            )
    for w, zw in enumerate((1, 2, 3, 5)):
        for tt in range(4):
            zz = 2 * tt + w // 2
            dst, rsem = RB.at[w % 2], r_recv.at[w % 2]
            if zz == zw:
                local(lt, dst, rsem, z == zw)
            else:
                send(
                    lambda dst=dst, tt=tt, rsem=rsem, zz=zz: copy_to(
                        lt, dst, r_send.at[tt], rsem, at(x, y, zz, k)
                    ),
                    z == zw,
                )

    def piece(j):
        return RX.at[pl.ds(j * RUN, RUN), :]

    for j in range(4):
        src = half(lt, j, RUN)
        local(src, piece(j), c_recv.at[j], z == 7)
        for i, zz in enumerate((0, 6)):
            send(
                lambda src=src, j=j, i=i, zz=zz: copy_to(
                    src, piece(j), c_send.at[2 * j + i], c_recv.at[j], at(x, y, zz, k)
                ),
                z == 7,
            )
    is_router = z == 6

    @pl.when(is_router)
    def _():
        RP[k * 4 + x] = lax.dot_general(rights[...], lt[...], NT, preferred_element_type=F32)

    for i in range(1, 8):
        dx, kk = i // 2, i % 2
        send(
            lambda i=i, dx=dx, kk=kk: copy_to(
                RP.at[k * 4 + x], RP.at[k * 4 + x], n_send.at[i - 1], n_recv.at[k * 4 + x],
                at(step(x, dx, 4), y, z, lax.rem(k + kk, 2)),
            ),
            is_router,
        )

    def left_arrive(p, hh):
        pltpu.make_async_copy(half(LB.at[p], hh), half(LB.at[p], hh), l_recv.at[2 * p + hh]).wait()

    role = step(y - t, 4, 4)
    for p in range(2):

        def both(cond, p=p):
            return cond if p == 0 else jnp.logical_and(cond, zl == 1)

        def arrivals(p=p):
            left_arrive(p, 0)
            left_arrive(p, 1)

        if p == 0:
            arrivals()
        else:
            pl.when(zl == 1)(arrivals)

        def on(i, hh, device, p=p):
            ref = half(LB.at[p], hh)
            return copy_to(ref, ref, b_send.at[4 * p + i], l_recv.at[2 * p + hh], device)

        for i, (hh, device) in enumerate(((0, north), (1, south), (1, north), (0, south))):
            send(lambda i=i, hh=hh, device=device, on=on: on(i, hh, device), both(role == 0))
        send(lambda on=on: on(0, 0, north), both(role == 1))
        send(lambda on=on: on(0, 1, south), both(role == 3))

    for j in range(2):
        pltpu.make_async_copy(RB.at[j], RB.at[j], r_recv.at[j]).wait()
        left = LB[zl * j]
        theirs = RB[j, pl.ds(pl.multiple_of((1 - k) * HALF, 16), HALF), :]
        PB[j] = lax.dot_general(left, theirs, NT, preferred_element_type=F32).astype(BF)
        send(lambda j=j: copy_to(PB.at[j], QB.at[j], d_send.at[j], d_recv.at[j], partner))
        ours = RB[j, pl.ds(pl.multiple_of(k * HALF, 16), HALF), :]
        SB[j] = lax.dot_general(left, ours, NT, preferred_element_type=F32)

    def quarter(ref, xx):
        return ref.at[pl.ds(pl.multiple_of(xx * RUN, 16), RUN), :]

    for j in range(2):
        copy_to(PB.at[j], QB.at[j], d_send.at[j], d_recv.at[j], partner).wait_recv()
        total = SB[j] + QB[j].astype(F32)
        SB[j] = total
        RSF[j] = total.astype(BF)
        for i, dx in enumerate((1, 3, 2)):
            xx = step(x, dx, 4)
            send(
                lambda j=j, i=i, xx=xx: copy_to(
                    quarter(RSF.at[j], xx), RSB.at[j, x], q_send.at[3 * j + i], q_recv.at[4 * j + x],
                    at(xx, y, z, k),
                )
            )

    goes_on = jnp.logical_or(z <= 2, jnp.logical_or(z == 5, z == 6))
    z_next = jnp.where(z <= 2, z + 1, z - 1)
    z_next = jnp.where(goes_on, z_next, step(z, 1, 8))
    for j in range(4):
        pltpu.make_async_copy(piece(j), piece(j), c_recv.at[j]).wait()
        send(
            lambda j=j: copy_to(piece(j), piece(j), c_send.at[j], c_recv.at[j], at(x, y, z_next, k)),
            goes_on,
        )

    def result(w, xx):
        return AO.at[w, pl.ds(pl.multiple_of(xx * RUN, 16), RUN), :]

    for j in range(2):
        total = SB[j, pl.ds(pl.multiple_of(x * RUN, 16), RUN), :]
        for dx in range(1, 4):
            xx = step(x, dx, 4)
            copy_to(RSB.at[j, xx], RSB.at[j, xx], q_send.at[0], q_recv.at[4 * j + xx], partner).wait_recv()
            total += RSB[j, xx].astype(F32)
        w = 2 * zl + j
        AO[w, pl.ds(pl.multiple_of(x * RUN, 16), RUN), :] = (RATE * total).astype(BF)
        for i, device in enumerate((pair, east, west, at(xo, y, z, k))):
            send(
                lambda w=w, i=i, j=j, device=device: copy_to(
                    result(w, x), result(w, x), g_send.at[4 * j + i], g_recv.at[4 * w + x], device
                )
            )

    def result_arrive(w, xx):
        copy_to(result(w, xx), result(w, xx), g_send.at[0], g_recv.at[4 * w + xx], partner).wait_recv()

    for j in range(2):
        w = 2 * (1 - zl) + j
        result_arrive(w, x)
        for i, device in enumerate((east, west, at(xo, y, z, k))):
            send(
                lambda w=w, i=i, j=j, device=device: copy_to(
                    result(w, x), result(w, x), g_send.at[8 + 3 * j + i], g_recv.at[4 * w + x], device
                )
            )

    own = RX.at[pl.ds(pl.multiple_of(k * HALF, 16), HALF), :]
    other = RX.at[pl.ds(pl.multiple_of((1 - k) * HALF, 16), HALF), :]
    pltpu.make_async_copy(own, EB.at[x, k], v_recv.at[0]).start()
    send(lambda: copy_to(other, EB.at[x, k], v_send.at[0], v_recv.at[1], partner))
    pltpu.make_async_copy(own, EB.at[x, k], v_recv.at[0]).wait()

    def embed_part(xx, kk, hh):
        return EB.at[xx, kk, pl.ds(hh * RUN, RUN), :]

    n_e = [0]

    def embed_on(xx, kk, hh, device):
        i = n_e[0]
        n_e[0] += 1
        ref = embed_part(xx, kk, hh)
        send(lambda: copy_to(ref, ref, e_send.at[i], e_recv.at[xx * 4 + kk * 2 + hh], device))

    def embed_arrive(xx, kk, hh):
        ref = embed_part(xx, kk, hh)
        copy_to(ref, ref, e_send.at[0], e_recv.at[xx * 4 + kk * 2 + hh], partner).wait_recv()

    for kk in (k, 1 - k):
        if kk is not k:
            copy_to(own, EB.at[x, kk], v_send.at[0], v_recv.at[1], partner).wait_recv()
        for hh, device in ((0, east), (1, west), (1, east), (0, west)):
            embed_on(x, kk, hh, device)
    for kk in (k, 1 - k):
        embed_arrive(xm, kk, 0)
        embed_on(xm, kk, 0, east)
        embed_arrive(xp, kk, 1)
        embed_on(xp, kk, 1, west)

    @pl.when(is_router)
    def _():
        for i in range(1, 8):
            ss = step(k * 4 + x, i, 8)
            copy_to(RP.at[ss], RP.at[ss], n_send.at[0], n_recv.at[ss], partner).wait_recv()
        total = jnp.zeros((8, WIDE), F32)
        for ss in range(8):
            total += RP[ss]
        RP[8] = RATE * total

    for dy in range(4):
        for zz in range(2):
            yy, z_to = step(y, dy, 4), 2 * y + zz
            cond = is_router
            if dy == 0 and zz == 0:
                stays = jnp.logical_and(is_router, y == 3)
                local(RP.at[8], router, w_recv.at[0], stays)
                cond = jnp.logical_and(is_router, y != 3)
            send(
                lambda dy=dy, zz=zz, yy=yy, z_to=z_to: copy_to(
                    RP.at[8], router, w_send.at[2 * dy + zz], w_recv.at[0], at(x, yy, z_to, k)
                ),
                cond,
            )

    for kk in (k, 1 - k):
        for xx, hh in ((xm, 1), (xp, 0), (xo, 0), (xo, 1)):
            embed_arrive(xx, kk, hh)
    for dx in (1, 3, 2):
        for w in range(4):
            result_arrive(w, step(x, dx, 4))
    pltpu.make_async_copy(router, router, w_recv.at[0]).wait()
    for cond, make in pending:
        if cond is None:
            make().wait_send()
        else:

            @pl.when(cond)
            def _(make=make):
                make().wait_send()


def combine(lt, rights):
    return pl.pallas_call(
        combine_kernel,
        out_shape=(
            jax.ShapeDtypeStruct((4, WIDE, HALF), BF),
            jax.ShapeDtypeStruct((4, 2, HALF, TOK), BF),
            jax.ShapeDtypeStruct((8, WIDE), F32),
        ),
        in_specs=[VM] * 2,
        out_specs=[VM] * 3,
        scratch_shapes=[
            pltpu.VMEM((2, WIDE, TOK), BF),
            pltpu.VMEM((2, WIDE, TOK), BF),
            pltpu.VMEM((WIDE, TOK), BF),
            pltpu.VMEM((2, WIDE, HALF), BF),
            pltpu.VMEM((2, WIDE, HALF), BF),
            pltpu.VMEM((2, WIDE, HALF), F32),
            pltpu.VMEM((2, WIDE, HALF), BF),
            pltpu.VMEM((2, 4, RUN, HALF), BF),
            pltpu.VMEM((9, 8, WIDE), F32),
        ]
        + [DMA((n,)) for n in (6, 4, 4, 2, 8, 8, 4, 2, 2, 6, 8, 14, 16, 12, 16, 1, 2, 7, 8, 8, 1)],
        compiler_params=pltpu.CompilerParams(
            collective_id=1, has_side_effects=True, vmem_limit_bytes=60 * 1024 * 1024
        ),
    )(lt, rights)


STEP = 512


def finish_kernel(AO, EB, router_in, ids, norms_in, diag, attn, embed, router, norms):
    i = pl.program_id(0)
    t = lax.axis_index("tensor")
    attn[...] = AO[...].astype(F32)
    router[...] = router_in[...]
    norms[...] = norms_in[...]
    start = (t * (8192 // 4) + i * STEP).astype(F32)
    vocab = lax.broadcasted_iota(jnp.int32, (STEP, TOK), 0).astype(F32) + start
    total = jnp.zeros((STEP, HALF), F32)
    counts = jnp.zeros((STEP, TOK), F32)
    for xx in range(4):
        for kk in range(2):
            hit = (vocab == ids[kk * 4 + xx : kk * 4 + xx + 1, :]).astype(F32)
            counts += hit
            total += lax.dot_general(hit.astype(BF), EB[xx, kk], NT, preferred_element_type=F32)
    count = jnp.sum(counts, axis=1, keepdims=True)
    divisor = 0.5 * diag[...] + (0.5 / TOKENS) * count + 0.01
    embed[...] = RATE * total / divisor


def finish(AO, EB, router, ids, norms, diag):
    whole = lambda a: pl.BlockSpec(a.shape, lambda i: (0,) * a.ndim)
    return pl.pallas_call(
        finish_kernel,
        grid=(4,),
        out_shape=(
            jax.ShapeDtypeStruct((4, WIDE, HALF), F32),
            jax.ShapeDtypeStruct((2048, HALF), F32),
            jax.ShapeDtypeStruct((8, WIDE), F32),
            jax.ShapeDtypeStruct((2, FEAT), F32),
        ),
        in_specs=[
            pl.BlockSpec((1, WIDE, HALF), lambda i: (i, 0, 0)),
            whole(EB),
            whole(router),
            whole(ids),
            whole(norms),
            pl.BlockSpec((STEP, 1), lambda i: (i, 0)),
        ],
        out_specs=[
            pl.BlockSpec((1, WIDE, HALF), lambda i: (i, 0, 0)),
            pl.BlockSpec((STEP, HALF), lambda i: (i, 0)),
            pl.BlockSpec((8, WIDE), lambda i: (0, 0)),
            pl.BlockSpec((2, FEAT), lambda i: (0, 0)),
        ],
    )(AO, EB, router, ids, norms, diag)


def per_device(
    activations,
    router_grad,
    token_ids,
    norm_terms,
    old_factors,
    old_router_factor,
    old_norm_diag,
    old_embed_diag,
):
    feats = jnp.transpose(activations, (0, 2, 1))
    old = jnp.transpose(old_factors[0].astype(BF))
    lt, rights, ids, norms = precondition(
        feats, old, router_grad, token_ids[None, :], norm_terms, old_router_factor, old_norm_diag
    )
    AO, EB, router = combine(lt, rights)
    attn, embed, router, norms = finish(AO, EB, router, ids, norms, old_embed_diag[:, None])
    return attn, router, norms, embed


def solution(mesh):
    return jax.shard_map(
        per_device,
        mesh=mesh,
        in_specs=(
            P(None, "shard", ("tensor", "section")),
            P(None, "shard"),
            P("shard"),
            P(None, "shard", ("tensor", "section")),
            P("shard", "tensor", "section"),
            P(),
            P(None, ("tensor", "section")),
            P("tensor"),
        ),
        out_specs=(
            P(None, "tensor", "section"),
            P(None, "tensor"),
            P(None, ("tensor", "section")),
            P("tensor", "section"),
        ),
        check_vma=False,
    )
```

time: 1100 us -> 223 us (0.20)
  the two profiles are of different devices: /device:TPU:120 before, /device:TPU:233 now
where the time goes in v1:
time: 223 us; the launch traced here: 222 us
  Pallas kernels  209 us (94%)
  local copies, waits for them, and re-layouts  10.9 us (5%)
    pallas_call x1, Pallas kernels, combine(): pl.pallas_call(combine_kernel, out_shape=(jax.ShapeDtypeStruct((4, WIDE,...  101 us
    pallas_call x1, Pallas kernels, precondition(): pl.pallas_call(precondition_kernel, out_shape=(jax.ShapeDtypeStruct((WIDE...  99 us
    unnamed x5, local copies, waits for them, and re-layouts  8.91 us
    pallas_call x1, Pallas kernels, finish(): pl.pallas_call(finish_kernel, grid=(4,), out_shape=(jax.ShapeDtypeStruct(...  8.47 us

profile of v1, /device:TPU:233, one launch (start us, length us, event | category | flops | bytes accessed | tf_op | source)
XLA Modules:
  0.0 222.3 jit_solution(15759860959595712899)
XLA Ops:
  0.6 1.6 copy.15.norm_terms
  2.3 1.9 convert_bitcast_fusion.old
  4.2 99.0 %shard_map.111 = (bf16[576,256]{1,0:T(8,128)(2,1)}, bf16[8,256]{1,0:T(8,128)(2,1)}, f32[8,256]{1,0:T(8,128)}, f32[2,72]{1,0:T(2,128)}) custom-call(bf16[8,72,256]{2,1,0:T(8,128)(2,1)} %bitcast.7, bf16[288,576]{1,0:T(8,128)(2,1)} %convert_bitcast_fusion.old, bf16[8,256]{1,0:T(8,128)(2,1)} %router_grad.1, s32[1,256]{1,0:T(1,128)} %bitcast.9, ...), custom_call_target="tpu_custom_call" | custom-call | tf_op jit(solution)/shard_map/pallas_call | solution.py:402
  103.2 2.0 copy.16.diag
  105.2 101.3 %shard_map.112 = (bf16[4,576,288]{2,1,0:T(8,128)(2,1)}, bf16[4,2,288,256]{3,2,1,0:T(8,128)(2,1)}, f32[8,576]{1,0:T(8,128)}) custom-call(bf16[576,256]{1,0:T(8,128)(2,1)} %get-tuple-element.15.lt, bf16[8,256]{1,0:T(8,128)(2,1)} %get-tuple-element.16.rights), custom_call_target="tpu_custom_call" | custom-call | tf_op jit(solution)/shard_map/pallas_call | solution.py:706
  206.6 8.5 %shard_map.113 = (f32[4,576,288]{2,1,0:T(8,128)}, f32[2048,288]{1,0:T(8,128)}, f32[8,576]{1,0:T(8,128)}, f32[2,72]{1,0:T(2,128)}) custom-call(bf16[4,576,288]{2,1,0:T(8,128)(2,1)} %get-tuple-element.17.AO, bf16[4,2,288,256]{3,2,1,0:T(8,128)(2,1)} %get-tuple-element.18.EB, f32[8,576]{1,0:T(8,128)} %get-tuple-element.19.router_in, ...), custom_call_target="tpu_custom_call" | custom-call | tf_op jit(solution)/shard_map/pallas_call | solution.py:758
  215.0 0.0 copy-start
  215.0 5.1 %copy.17 = f32[4,576,288]{1,2,0:T(8,128)} copy(f32[4,576,288]{2,1,0:T(8,128)} %get-tuple-element.30) | data formatting | bytes 5308416
  220.2 0.0 copy-done
  220.2 2.1 copy.18
Async XLA Ops:
  215.0 5.1 %copy-start = (f32[2048,288]{1,0:T(8,128)S(1)}, f32[2048,288]{1,0:T(8,128)}, u32[]{:S(2)}) copy-start(f32[2048,288]{1,0:T(8,128)} %get-tuple-element.33) | copy-start | bytes 7077892

commit v2 on v1

--- a/solution.py
+++ b/solution.py
@@ -534,6 +534,16 @@
             is_router,
         )
 
+    goes_on = jnp.logical_or(z <= 2, jnp.logical_or(z == 5, z == 6))
+    z_next = jnp.where(z <= 2, z + 1, z - 1)
+    z_next = jnp.where(goes_on, z_next, step(z, 1, 8))
+    for j in range(4):
+        pltpu.make_async_copy(piece(j), piece(j), c_recv.at[j]).wait()
+        send(
+            lambda j=j: copy_to(piece(j), piece(j), c_send.at[j], c_recv.at[j], at(x, y, z_next, k)),
+            goes_on,
+        )
+
     def left_arrive(p, hh):
         pltpu.make_async_copy(half(LB.at[p], hh), half(LB.at[p], hh), l_recv.at[2 * p + hh]).wait()
 
@@ -561,17 +571,43 @@
         send(lambda on=on: on(0, 0, north), both(role == 1))
         send(lambda on=on: on(0, 1, south), both(role == 3))
 
+    own = RX.at[pl.ds(pl.multiple_of(k * HALF, 16), HALF), :]
+    other = RX.at[pl.ds(pl.multiple_of((1 - k) * HALF, 16), HALF), :]
+    pltpu.make_async_copy(own, EB.at[x, k], v_recv.at[0]).start()
+    send(lambda: copy_to(other, EB.at[x, k], v_send.at[0], v_recv.at[1], partner))
+    pltpu.make_async_copy(own, EB.at[x, k], v_recv.at[0]).wait()
+
+    def embed_part(xx, kk, hh):
+        return EB.at[xx, kk, pl.ds(hh * RUN, RUN), :]
+
+    n_e = [0]
+
+    def embed_on(xx, kk, hh, device):
+        i = n_e[0]
+        n_e[0] += 1
+        ref = embed_part(xx, kk, hh)
+        send(lambda: copy_to(ref, ref, e_send.at[i], e_recv.at[xx * 4 + kk * 2 + hh], device))
+
+    def embed_arrive(xx, kk, hh):
+        ref = embed_part(xx, kk, hh)
+        copy_to(ref, ref, e_send.at[0], e_recv.at[xx * 4 + kk * 2 + hh], partner).wait_recv()
+
+    for kk in (k, 1 - k):
+        if kk is not k:
+            copy_to(own, EB.at[x, kk], v_send.at[0], v_recv.at[1], partner).wait_recv()
+        for hh, device in ((0, east), (1, west), (1, east), (0, west)):
+            embed_on(x, kk, hh, device)
     for j in range(2):
         pltpu.make_async_copy(RB.at[j], RB.at[j], r_recv.at[j]).wait()
         left = LB[zl * j]
         theirs = RB[j, pl.ds(pl.multiple_of((1 - k) * HALF, 16), HALF), :]
-        PB[j] = lax.dot_general(left, theirs, NT, preferred_element_type=F32).astype(BF)
+        PB[j] = lax.dot_general(theirs, left, NT, preferred_element_type=F32).astype(BF)
         send(lambda j=j: copy_to(PB.at[j], QB.at[j], d_send.at[j], d_recv.at[j], partner))
         ours = RB[j, pl.ds(pl.multiple_of(k * HALF, 16), HALF), :]
-        SB[j] = lax.dot_general(left, ours, NT, preferred_element_type=F32)
+        SB[j] = lax.dot_general(ours, left, NT, preferred_element_type=F32)
 
     def quarter(ref, xx):
-        return ref.at[pl.ds(pl.multiple_of(xx * RUN, 16), RUN), :]
+        return ref.at[pl.ds(pl.multiple_of(xx * FEAT, 8), FEAT), :]
 
     for j in range(2):
         copy_to(PB.at[j], QB.at[j], d_send.at[j], d_recv.at[j], partner).wait_recv()
@@ -587,31 +623,27 @@
                 )
             )
 
-    goes_on = jnp.logical_or(z <= 2, jnp.logical_or(z == 5, z == 6))
-    z_next = jnp.where(z <= 2, z + 1, z - 1)
-    z_next = jnp.where(goes_on, z_next, step(z, 1, 8))
-    for j in range(4):
-        pltpu.make_async_copy(piece(j), piece(j), c_recv.at[j]).wait()
-        send(
-            lambda j=j: copy_to(piece(j), piece(j), c_send.at[j], c_recv.at[j], at(x, y, z_next, k)),
-            goes_on,
-        )
+    for kk in (k, 1 - k):
+        embed_arrive(xm, kk, 0)
+        embed_on(xm, kk, 0, east)
+        embed_arrive(xp, kk, 1)
+        embed_on(xp, kk, 1, west)
 
     def result(w, xx):
-        return AO.at[w, pl.ds(pl.multiple_of(xx * RUN, 16), RUN), :]
+        return AO.at[w, pl.ds(pl.multiple_of(xx * FEAT, 8), FEAT), :]
 
     for j in range(2):
-        total = SB[j, pl.ds(pl.multiple_of(x * RUN, 16), RUN), :]
+        total = SB[j, pl.ds(pl.multiple_of(x * FEAT, 8), FEAT), :]
         for dx in range(1, 4):
             xx = step(x, dx, 4)
             copy_to(RSB.at[j, xx], RSB.at[j, xx], q_send.at[0], q_recv.at[4 * j + xx], partner).wait_recv()
             total += RSB[j, xx].astype(F32)
         w = 2 * zl + j
-        AO[w, pl.ds(pl.multiple_of(x * RUN, 16), RUN), :] = (RATE * total).astype(BF)
-        for i, device in enumerate((pair, east, west, at(xo, y, z, k))):
+        AO[w, pl.ds(pl.multiple_of(x * FEAT, 8), FEAT), :] = (RATE * total).astype(BF)
+        for i, device in enumerate((pair, east, west)):
             send(
                 lambda w=w, i=i, j=j, device=device: copy_to(
-                    result(w, x), result(w, x), g_send.at[4 * j + i], g_recv.at[4 * w + x], device
+                    result(w, x), result(w, x), g_send.at[3 * j + i], g_recv.at[4 * w + x], device
                 )
             )
 
@@ -621,44 +653,25 @@
     for j in range(2):
         w = 2 * (1 - zl) + j
         result_arrive(w, x)
-        for i, device in enumerate((east, west, at(xo, y, z, k))):
+        for i, device in enumerate((east, west)):
             send(
                 lambda w=w, i=i, j=j, device=device: copy_to(
-                    result(w, x), result(w, x), g_send.at[8 + 3 * j + i], g_recv.at[4 * w + x], device
+                    result(w, x), result(w, x), g_send.at[6 + 2 * j + i], g_recv.at[4 * w + x], device
                 )
             )
 
-    own = RX.at[pl.ds(pl.multiple_of(k * HALF, 16), HALF), :]
-    other = RX.at[pl.ds(pl.multiple_of((1 - k) * HALF, 16), HALF), :]
-    pltpu.make_async_copy(own, EB.at[x, k], v_recv.at[0]).start()
-    send(lambda: copy_to(other, EB.at[x, k], v_send.at[0], v_recv.at[1], partner))
-    pltpu.make_async_copy(own, EB.at[x, k], v_recv.at[0]).wait()
-
-    def embed_part(xx, kk, hh):
-        return EB.at[xx, kk, pl.ds(hh * RUN, RUN), :]
-
-    n_e = [0]
-
-    def embed_on(xx, kk, hh, device):
-        i = n_e[0]
-        n_e[0] += 1
-        ref = embed_part(xx, kk, hh)
-        send(lambda: copy_to(ref, ref, e_send.at[i], e_recv.at[xx * 4 + kk * 2 + hh], device))
-
-    def embed_arrive(xx, kk, hh):
-        ref = embed_part(xx, kk, hh)
-        copy_to(ref, ref, e_send.at[0], e_recv.at[xx * 4 + kk * 2 + hh], partner).wait_recv()
-
-    for kk in (k, 1 - k):
-        if kk is not k:
-            copy_to(own, EB.at[x, kk], v_send.at[0], v_recv.at[1], partner).wait_recv()
-        for hh, device in ((0, east), (1, west), (1, east), (0, west)):
-            embed_on(x, kk, hh, device)
-    for kk in (k, 1 - k):
-        embed_arrive(xm, kk, 0)
-        embed_on(xm, kk, 0, east)
-        embed_arrive(xp, kk, 1)
-        embed_on(xp, kk, 1, west)
+    def result_part(w, xx, hh):
+        return AO.at[w, pl.ds(pl.multiple_of(xx * FEAT + hh * 40, 8), (40, 32)[hh]), :]
+
+    for i, w in enumerate((2 * zl, 2 * zl + 1, 2 * (1 - zl), 2 * (1 - zl) + 1)):
+        for hh, xx, device in ((0, xm, east), (1, xp, west)):
+            result_arrive(w, xx)
+            send(
+                lambda w=w, i=i, hh=hh, xx=xx, device=device: copy_to(
+                    result_part(w, xx, hh), result_part(w, xx, hh), g_send.at[10 + 2 * i + hh],
+                    g_recv.at[16 + 2 * w + hh], device,
+                )
+            )
 
     @pl.when(is_router)
     def _():
@@ -688,9 +701,10 @@
     for kk in (k, 1 - k):
         for xx, hh in ((xm, 1), (xp, 0), (xo, 0), (xo, 1)):
             embed_arrive(xx, kk, hh)
-    for dx in (1, 3, 2):
-        for w in range(4):
-            result_arrive(w, step(x, dx, 4))
+    for w in range(4):
+        for hh in range(2):
+            ref = result_part(w, xo, hh)
+            copy_to(ref, ref, g_send.at[0], g_recv.at[16 + 2 * w + hh], partner).wait_recv()
     pltpu.make_async_copy(router, router, w_recv.at[0]).wait()
     for cond, make in pending:
         if cond is None:
@@ -706,7 +720,7 @@
     return pl.pallas_call(
         combine_kernel,
         out_shape=(
-            jax.ShapeDtypeStruct((4, WIDE, HALF), BF),
+            jax.ShapeDtypeStruct((4, HALF, WIDE), BF),
             jax.ShapeDtypeStruct((4, 2, HALF, TOK), BF),
             jax.ShapeDtypeStruct((8, WIDE), F32),
         ),
@@ -716,14 +730,14 @@
             pltpu.VMEM((2, WIDE, TOK), BF),
             pltpu.VMEM((2, WIDE, TOK), BF),
             pltpu.VMEM((WIDE, TOK), BF),
-            pltpu.VMEM((2, WIDE, HALF), BF),
-            pltpu.VMEM((2, WIDE, HALF), BF),
-            pltpu.VMEM((2, WIDE, HALF), F32),
-            pltpu.VMEM((2, WIDE, HALF), BF),
-            pltpu.VMEM((2, 4, RUN, HALF), BF),
+            pltpu.VMEM((2, HALF, WIDE), BF),
+            pltpu.VMEM((2, HALF, WIDE), BF),
+            pltpu.VMEM((2, HALF, WIDE), F32),
+            pltpu.VMEM((2, HALF, WIDE), BF),
+            pltpu.VMEM((2, 4, FEAT, WIDE), BF),
             pltpu.VMEM((9, 8, WIDE), F32),
         ]
-        + [DMA((n,)) for n in (6, 4, 4, 2, 8, 8, 4, 2, 2, 6, 8, 14, 16, 12, 16, 1, 2, 7, 8, 8, 1)],
+        + [DMA((n,)) for n in (6, 4, 4, 2, 8, 8, 4, 2, 2, 6, 8, 18, 24, 12, 16, 1, 2, 7, 8, 8, 1)],
         compiler_params=pltpu.CompilerParams(
             collective_id=1, has_side_effects=True, vmem_limit_bytes=60 * 1024 * 1024
         ),
@@ -741,16 +755,17 @@
     norms[...] = norms_in[...]
     start = (t * (8192 // 4) + i * STEP).astype(F32)
     vocab = lax.broadcasted_iota(jnp.int32, (STEP, TOK), 0).astype(F32) + start
-    total = jnp.zeros((STEP, HALF), F32)
+    total = jnp.zeros((HALF, STEP), F32)
     counts = jnp.zeros((STEP, TOK), F32)
     for xx in range(4):
         for kk in range(2):
             hit = (vocab == ids[kk * 4 + xx : kk * 4 + xx + 1, :]).astype(F32)
             counts += hit
-            total += lax.dot_general(hit.astype(BF), EB[xx, kk], NT, preferred_element_type=F32)
-    count = jnp.sum(counts, axis=1, keepdims=True)
+            total += lax.dot_general(EB[xx, kk], hit.astype(BF), NT, preferred_element_type=F32)
+    ones = jnp.ones((8, TOK), BF)
+    count = lax.dot_general(ones, counts.astype(BF), NT, preferred_element_type=F32)[0:1, :]
     divisor = 0.5 * diag[...] + (0.5 / TOKENS) * count + 0.01
-    embed[...] = RATE * total / divisor
+    embed[...] = total * (RATE / divisor)
 
 
 def finish(AO, EB, router, ids, norms, diag):
@@ -759,22 +774,22 @@
         finish_kernel,
         grid=(4,),
         out_shape=(
-            jax.ShapeDtypeStruct((4, WIDE, HALF), F32),
-            jax.ShapeDtypeStruct((2048, HALF), F32),
+            jax.ShapeDtypeStruct((4, HALF, WIDE), F32),
+            jax.ShapeDtypeStruct((HALF, 2048), F32),
             jax.ShapeDtypeStruct((8, WIDE), F32),
             jax.ShapeDtypeStruct((2, FEAT), F32),
         ),
         in_specs=[
-            pl.BlockSpec((1, WIDE, HALF), lambda i: (i, 0, 0)),
+            pl.BlockSpec((1, HALF, WIDE), lambda i: (i, 0, 0)),
             whole(EB),
             whole(router),
             whole(ids),
             whole(norms),
-            pl.BlockSpec((STEP, 1), lambda i: (i, 0)),
+            pl.BlockSpec((1, STEP), lambda i: (0, i)),
         ],
         out_specs=[
-            pl.BlockSpec((1, WIDE, HALF), lambda i: (i, 0, 0)),
-            pl.BlockSpec((STEP, HALF), lambda i: (i, 0)),
+            pl.BlockSpec((1, HALF, WIDE), lambda i: (i, 0, 0)),
+            pl.BlockSpec((HALF, STEP), lambda i: (0, i)),
             pl.BlockSpec((8, WIDE), lambda i: (0, 0)),
             pl.BlockSpec((2, FEAT), lambda i: (0, 0)),
         ],
@@ -797,8 +812,8 @@
         feats, old, router_grad, token_ids[None, :], norm_terms, old_router_factor, old_norm_diag
     )
     AO, EB, router = combine(lt, rights)
-    attn, embed, router, norms = finish(AO, EB, router, ids, norms, old_embed_diag[:, None])
-    return attn, router, norms, embed
+    attn, embed, router, norms = finish(AO, EB, router, ids, norms, old_embed_diag[None, :])
+    return jnp.transpose(attn, (0, 2, 1)), router, norms, jnp.transpose(embed)
 
 
 def solution(mesh):

time: 223 us -> 212 us (0.951)
  the two profiles are of different devices: /device:TPU:233 before, /device:TPU:120 now
where the time goes in v2:
time: 212 us; the launch traced here: 211 us
  Pallas kernels  207 us (98%)
    pallas_call x1, Pallas kernels, precondition(): pl.pallas_call(precondition_kernel, out_shape=(jax.ShapeDtypeStruct((WIDE...  108 us
    pallas_call x1, Pallas kernels, combine(): pl.pallas_call(combine_kernel, out_shape=(jax.ShapeDtypeStruct((4, HALF,...  92.8 us
    pallas_call x1, Pallas kernels, finish(): pl.pallas_call(finish_kernel, grid=(4,), out_shape=(jax.ShapeDtypeStruct(...  6.61 us

profile of v2, /device:TPU:120, one launch (start us, length us, event | category | flops | bytes accessed | tf_op | source)
XLA Modules:
  0.0 211.5 jit_solution(5472709004102042695)
XLA Ops:
  0.6 1.6 copy.12.norm_terms
  2.3 1.9 convert_bitcast_fusion.old
  4.2 107.9 %shard_map.111 = (bf16[576,256]{1,0:T(8,128)(2,1)}, bf16[8,256]{1,0:T(8,128)(2,1)}, f32[8,256]{1,0:T(8,128)}, f32[2,72]{1,0:T(2,128)}) custom-call(bf16[8,72,256]{2,1,0:T(8,128)(2,1)} %bitcast.9, bf16[288,576]{1,0:T(8,128)(2,1)} %convert_bitcast_fusion.old, bf16[8,256]{1,0:T(8,128)(2,1)} %router_grad.1, s32[1,256]{1,0:T(1,128)} %bitcast.11, ...), custom_call_target="tpu_custom_call" | custom-call | tf_op jit(solution)/shard_map/pallas_call | solution.py:402
  112.1 92.8 %shard_map.112 = (bf16[4,288,576]{2,1,0:T(8,128)(2,1)}, bf16[4,2,288,256]{3,2,1,0:T(8,128)(2,1)}, f32[8,576]{1,0:T(8,128)}) custom-call(bf16[576,256]{1,0:T(8,128)(2,1)} %get-tuple-element.15.lt, bf16[8,256]{1,0:T(8,128)(2,1)} %get-tuple-element.16.rights), custom_call_target="tpu_custom_call" | custom-call | tf_op jit(solution)/shard_map/pallas_call | solution.py:720
  204.9 6.6 %shard_map.113 = (f32[4,288,576]{2,1,0:T(8,128)}, f32[288,2048]{1,0:T(8,128)}, f32[8,576]{1,0:T(8,128)}, f32[2,72]{1,0:T(2,128)}) custom-call(bf16[4,288,576]{2,1,0:T(8,128)(2,1)} %get-tuple-element.17.AO, bf16[4,2,288,256]{3,2,1,0:T(8,128)(2,1)} %get-tuple-element.18.EB, f32[8,576]{1,0:T(8,128)} %get-tuple-element.19.router_in, ...), custom_call_target="tpu_custom_call" | custom-call | tf_op jit(solution)/shard_map/pallas_call | solution.py:773

commit v3 on v2

--- a/solution.py
+++ b/solution.py
@@ -91,7 +91,15 @@
         signal(barrier, partner)
         signal(barrier, partner)
 
-    pl.semaphore_wait(barrier, 15 + 5 + 7 + 2)
+    for dy in range(4):
+        for dz in range(8):
+            if dy or dz:
+                signal(barrier, at(x, step(y, dy, 4), step(z, dz, 8), k))
+    for dx in range(4):
+        for kk in range(2):
+            if dx or kk:
+                signal(barrier, at(step(x, dx, 4), y, z, lax.rem(k + kk, 2)))
+    pl.semaphore_wait(barrier, 15 + 5 + 7 + 2 + 31 + 7)
 
     waits = []
 
@@ -300,13 +308,38 @@
         cp.start()
         waits.append(cp)
 
-    def times_matrix(block_of):
-        total = jnp.zeros((WIDE, TOK), F32)
-        for tt in range(4):
-            total += jnp.dot(MB[tt], block_of(tt), preferred_element_type=F32)
-        return total
-
-    def spread(r):
+    def shared_values():
+        for d in range(8):
+            ss = step(s, d, 8)
+            copy_to(small, small_all.at[ss], s_send.at[0], s_recv.at[ss], partner).wait_recv()
+
+        sums = jnp.zeros((EXPERTS, EXPERTS), F32)
+        stats = jnp.zeros((8, TOK), F32)
+        for ss in range(8):
+            grad = small_all[ss, 0:8, :].astype(BF)
+            sums += lax.dot_general(grad, grad, NT, preferred_element_type=F32)
+            stats += small_all[ss, 16:24, :]
+            all_ids[ss : ss + 1, :] = small_all[ss, 8:9, :]
+        norms[...] = RATE * stats[0:2, 0:FEAT] / (
+            0.5 * old_norm[...] + (0.5 / TOKENS) * stats[2:4, 0:FEAT] + 0.01
+        )
+        eye8 = (
+            lax.broadcasted_iota(jnp.int32, (8, 8), 0) == lax.broadcasted_iota(jnp.int32, (8, 8), 1)
+        ).astype(F32)
+        matrix8 = 0.5 * old_router[...] + (0.5 / TOKENS) * sums + 0.01 * eye8
+        scale8 = EXPERTS / (3.0 * jnp.sum(jnp.sum(matrix8 * eye8, axis=1, keepdims=True), axis=0, keepdims=True))
+        low8 = matrix8.astype(BF)
+        first8 = 2.0 * scale8 * eye8 - scale8 * scale8 * low8.astype(F32)
+        image8 = jnp.dot(low8, first8.astype(BF), preferred_element_type=F32).astype(BF)
+        inverse8 = (
+            2.0 * first8 - jnp.dot(first8.astype(BF), image8, preferred_element_type=F32)
+        ).astype(BF)
+        mine = small_all[k * 4 + x, 0:8, :].astype(BF)
+        rights[...] = lax.dot_general(
+            inverse8, mine, (((0,), (0,)), ((), ())), preferred_element_type=F32
+        ).astype(BF)
+
+    def spread_times(r):
         def part(yy, hh):
             return UB.at[r, yy, pl.ds(hh * HALF, HALF), :]
 
@@ -320,28 +353,37 @@
             ref = part(yy, hh)
             copy_to(ref, ref, u_send.at[0], u_recv.at[8 * r + 2 * yy + hh], partner).wait_recv()
 
+        def term(yy):
+            return jnp.dot(MB[yy], UB[r, yy], preferred_element_type=F32)
+
         put(0, y, 0, north)
         put(1, y, 1, south)
         put(2, y, 1, north)
         put(3, y, 0, south)
+        total = term(y)
+        if r == 0:
+            shared_values()
         got(ym, 0)
         put(4, ym, 0, north)
         got(yp, 1)
         put(5, yp, 1, south)
         got(ym, 1)
+        total += term(ym)
         got(yp, 0)
+        total += term(yp)
         got(yo, 0)
         got(yo, 1)
-
-    u = times_matrix(lambda tt: AT[x, pl.ds(tt * WIDE, WIDE), :])
+        return total + term(yo)
+
+    u = jnp.zeros((WIDE, TOK), F32)
+    for tt in range(4):
+        u += jnp.dot(MB[tt], AT[x, pl.ds(tt * WIDE, WIDE), :], preferred_element_type=F32)
     UF[0] = u
     UB[0, y] = u.astype(BF)
-    spread(0)
-    u = times_matrix(lambda tt: UB[0, tt])
+    u = spread_times(0)
     UF[1] = u
     UB[1, y] = u.astype(BF)
-    spread(1)
-    u = times_matrix(lambda tt: UB[1, tt])
+    u = spread_times(1)
     for dd in range(1, 4):
         yy = step(y, dd, 4)
         copy_to(TR.at[yy], TR.at[yy], t_send.at[0], t_recv.at[yy], partner).wait_recv()
@@ -352,81 +394,23 @@
         scale * (4.0 * first - scale * (6.0 * UF[0] - scale * (4.0 * UF[1] - scale * u)))
     ).astype(BF)
 
-    for cp in waits:
-        cp.wait_send()
-
-    @pl.when(k != zl)
-    def _():
-        copy_to(feats.at[z], feats.at[z], z_send.at[0], z_recv.at[0], partner).wait_send()
-
-    @pl.when(jnp.logical_not(old_stays))
-    def _():
-        copy_to(old, old_block(0, 0), o_send.at[0], o_recv.at[0], partner).wait_send()
-
-    for d in range(8):
-        ss = step(s, d, 8)
-        copy_to(small, small_all.at[ss], s_send.at[0], s_recv.at[ss], partner).wait_recv()
-
-    sums = jnp.zeros((EXPERTS, EXPERTS), F32)
-    stats = jnp.zeros((8, TOK), F32)
-    for ss in range(8):
-        grad = small_all[ss, 0:8, :].astype(BF)
-        sums += lax.dot_general(grad, grad, NT, preferred_element_type=F32)
-        stats += small_all[ss, 16:24, :]
-        all_ids[ss : ss + 1, :] = small_all[ss, 8:9, :]
-    norms[...] = RATE * stats[0:2, 0:FEAT] / (
-        0.5 * old_norm[...] + (0.5 / TOKENS) * stats[2:4, 0:FEAT] + 0.01
-    )
-    eye8 = (
-        lax.broadcasted_iota(jnp.int32, (8, 8), 0) == lax.broadcasted_iota(jnp.int32, (8, 8), 1)
-    ).astype(F32)
-    matrix8 = 0.5 * old_router[...] + (0.5 / TOKENS) * sums + 0.01 * eye8
-    scale8 = EXPERTS / (3.0 * jnp.sum(jnp.sum(matrix8 * eye8, axis=1, keepdims=True), axis=0, keepdims=True))
-    low8 = matrix8.astype(BF)
-    first8 = 2.0 * scale8 * eye8 - scale8 * scale8 * low8.astype(F32)
-    image8 = jnp.dot(low8, first8.astype(BF), preferred_element_type=F32).astype(BF)
-    inverse8 = (
-        2.0 * first8 - jnp.dot(first8.astype(BF), image8, preferred_element_type=F32)
-    ).astype(BF)
-    mine = small_all[k * 4 + x, 0:8, :].astype(BF)
-    rights[...] = lax.dot_general(
-        inverse8, mine, (((0,), (0,)), ((), ())), preferred_element_type=F32
-    ).astype(BF)
+    def settle():
+        for cp in waits:
+            cp.wait_send()
+
+        @pl.when(k != zl)
+        def _():
+            copy_to(feats.at[z], feats.at[z], z_send.at[0], z_recv.at[0], partner).wait_send()
+
+        @pl.when(jnp.logical_not(old_stays))
+        def _():
+            copy_to(old, old_block(0, 0), o_send.at[0], o_recv.at[0], partner).wait_send()
+
+    return settle
 
 
 DMA = pltpu.SemaphoreType.DMA
 VM = pl.BlockSpec(memory_space=pltpu.VMEM)
-
-
-def precondition(*operands):
-    return pl.pallas_call(
-        precondition_kernel,
-        out_shape=(
-            jax.ShapeDtypeStruct((WIDE, TOK), BF),
-            jax.ShapeDtypeStruct((8, TOK), BF),
-            jax.ShapeDtypeStruct((8, TOK), F32),
-            jax.ShapeDtypeStruct((2, FEAT), F32),
-        ),
-        in_specs=[VM] * 7,
-        out_specs=[VM] * 4,
-        scratch_shapes=[
-            pltpu.VMEM((24, TOK), F32),
-            pltpu.VMEM((8, 24, TOK), F32),
-            pltpu.VMEM((4, D, TOK), BF),
-            pltpu.VMEM((4, WIDE, WIDE), BF),
-            pltpu.VMEM((4, WIDE, WIDE), F32),
-            pltpu.VMEM((4, WIDE, WIDE), BF),
-            pltpu.VMEM((4, WIDE, WIDE), BF),
-            pltpu.VMEM((4, WIDE, WIDE), BF),
-            pltpu.VMEM((2, 4, WIDE, TOK), BF),
-            pltpu.VMEM((2, WIDE, TOK), F32),
-            pltpu.VMEM((4, 8, 128), F32),
-        ]
-        + [DMA((n,)) for n in (8, 8, 1, 1, 6, 8, 4, 4, 60, 64, 4, 4, 12, 16, 3, 4, 7, 8)],
-        compiler_params=pltpu.CompilerParams(
-            collective_id=0, has_side_effects=True, vmem_limit_bytes=60 * 1024 * 1024
-        ),
-    )(*operands)
 
 
 def combine_kernel(
@@ -445,17 +429,6 @@
     partner = at(x, y, z, 1 - k)
     pair = at(x, y, 2 * t + 1 - zl, k)
 
-    barrier = pltpu.get_barrier_semaphore()
-    for dy in range(4):
-        for dz in range(8):
-            if dy or dz:
-                signal(barrier, at(x, step(y, dy, 4), step(z, dz, 8), k))
-    for dx in range(4):
-        for kk in range(2):
-            if dx or kk:
-                signal(barrier, at(step(x, dx, 4), y, z, lax.rem(k + kk, 2)))
-    pl.semaphore_wait(barrier, 31 + 7)
-
     pending = []
 
     def send(make, cond=None):
@@ -491,19 +464,38 @@
                 ),
                 cond,
             )
-    for w, zw in enumerate((1, 2, 3, 5)):
-        for tt in range(4):
-            zz = 2 * tt + w // 2
-            dst, rsem = RB.at[w % 2], r_recv.at[w % 2]
-            if zz == zw:
-                local(lt, dst, rsem, z == zw)
-            else:
+    for w, (zw, first) in enumerate(((1, (2, 0)), (2, (4, 0)), (3, (5, 1)), (5, (7, 3)))):
+        j = w % 2
+        for hh in range(2):
+            src, dst, rsem = half(lt, hh), half(RB.at[j], hh), r_recv.at[2 * j + hh]
+            if w:
+                local(src, dst, rsem, z == zw)
+            for i, zz in enumerate(first):
                 send(
-                    lambda dst=dst, tt=tt, rsem=rsem, zz=zz: copy_to(
-                        lt, dst, r_send.at[tt], rsem, at(x, y, zz, k)
+                    lambda src=src, dst=dst, rsem=rsem, i=i, hh=hh, zz=zz: copy_to(
+                        src, dst, r_send.at[2 * hh + i], rsem, at(x, y, zz, k)
                     ),
                     z == zw,
                 )
+
+    def right_arrive(j, hh):
+        ref = half(RB.at[j], hh)
+        pltpu.make_async_copy(ref, ref, r_recv.at[2 * j + hh]).wait()
+
+    def right_on(j, hh, cond, to):
+        pl.when(cond)(lambda: right_arrive(j, hh))
+        ref = half(RB.at[j], hh)
+        send(
+            lambda: copy_to(ref, ref, r_send.at[4 + 2 * j + hh], r_recv.at[2 * j + hh], at(x, y, to, k)),
+            cond,
+        )
+
+    def among(*planes):
+        found = z == planes[0]
+        for p in planes[1:]:
+            found = jnp.logical_or(found, z == p)
+        return found
+
 
     def piece(j):
         return RX.at[pl.ds(j * RUN, RUN), :]
@@ -544,6 +536,12 @@
             goes_on,
         )
 
+    on00, on01, on10, on11 = among(0, 2, 5), among(0, 1, 6), among(3, 4), among(0, 7)
+    right_on(0, 0, on00, jnp.where(z == 0, 6, jnp.where(z == 2, 4, 7)))
+    right_on(1, 0, on10, jnp.where(z == 4, 6, 1))
+    right_on(1, 1, on11, jnp.where(z == 0, 6, 1))
+    right_on(0, 1, on01, jnp.where(z == 0, 6, jnp.where(z == 1, 7, 4)))
+
     def left_arrive(p, hh):
         pltpu.make_async_copy(half(LB.at[p], hh), half(LB.at[p], hh), l_recv.at[2 * p + hh]).wait()
 
@@ -598,7 +596,9 @@
         for hh, device in ((0, east), (1, west), (1, east), (0, west)):
             embed_on(x, kk, hh, device)
     for j in range(2):
-        pltpu.make_async_copy(RB.at[j], RB.at[j], r_recv.at[j]).wait()
+        for hh in range(2):
+            done = ((on00, on01), (on10, on11))[j][hh]
+            pl.when(jnp.logical_not(done))(lambda j=j, hh=hh: right_arrive(j, hh))
         left = LB[zl * j]
         theirs = RB[j, pl.ds(pl.multiple_of((1 - k) * HALF, 16), HALF), :]
         PB[j] = lax.dot_general(theirs, left, NT, preferred_element_type=F32).astype(BF)
@@ -716,32 +716,64 @@
                 make().wait_send()
 
 
-def combine(lt, rights):
+PRE_SEMS = (8, 8, 1, 1, 6, 8, 4, 4, 60, 64, 4, 4, 12, 16, 3, 4, 7, 8)
+COMBINE_SEMS = (6, 4, 8, 4, 8, 8, 4, 2, 2, 6, 8, 18, 24, 12, 16, 1, 2, 7, 8, 8, 1)
+PRE_BUFFERS = (
+    ((24, TOK), F32),
+    ((8, 24, TOK), F32),
+    ((4, D, TOK), BF),
+    ((4, WIDE, WIDE), BF),
+    ((4, WIDE, WIDE), F32),
+    ((4, WIDE, WIDE), BF),
+    ((4, WIDE, WIDE), BF),
+    ((4, WIDE, WIDE), BF),
+    ((2, 4, WIDE, TOK), BF),
+    ((2, WIDE, TOK), F32),
+    ((4, 8, 128), F32),
+)
+COMBINE_BUFFERS = (
+    ((2, WIDE, TOK), BF),
+    ((2, WIDE, TOK), BF),
+    ((WIDE, TOK), BF),
+    ((2, HALF, WIDE), BF),
+    ((2, HALF, WIDE), BF),
+    ((2, HALF, WIDE), F32),
+    ((2, HALF, WIDE), BF),
+    ((2, 4, FEAT, WIDE), BF),
+    ((9, 8, WIDE), F32),
+)
+
+
+def update_kernel(*refs):
+    n = len(PRE_BUFFERS) + len(PRE_SEMS)
+    operands, (AO, EB, router, all_ids, norms) = refs[:7], refs[7:12]
+    lt, rights = refs[12:14]
+    settle = precondition_kernel(*operands, lt, rights, all_ids, norms, *refs[14 : 14 + n])
+    combine_kernel(lt, rights, AO, EB, router, *refs[14 + n :])
+    settle()
+
+
+def update(*operands):
     return pl.pallas_call(
-        combine_kernel,
+        update_kernel,
         out_shape=(
             jax.ShapeDtypeStruct((4, HALF, WIDE), BF),
             jax.ShapeDtypeStruct((4, 2, HALF, TOK), BF),
             jax.ShapeDtypeStruct((8, WIDE), F32),
+            jax.ShapeDtypeStruct((8, TOK), F32),
+            jax.ShapeDtypeStruct((2, FEAT), F32),
         ),
-        in_specs=[VM] * 2,
-        out_specs=[VM] * 3,
-        scratch_shapes=[
-            pltpu.VMEM((2, WIDE, TOK), BF),
-            pltpu.VMEM((2, WIDE, TOK), BF),
-            pltpu.VMEM((WIDE, TOK), BF),
-            pltpu.VMEM((2, HALF, WIDE), BF),
-            pltpu.VMEM((2, HALF, WIDE), BF),
-            pltpu.VMEM((2, HALF, WIDE), F32),
-            pltpu.VMEM((2, HALF, WIDE), BF),
-            pltpu.VMEM((2, 4, FEAT, WIDE), BF),
-            pltpu.VMEM((9, 8, WIDE), F32),
-        ]
-        + [DMA((n,)) for n in (6, 4, 4, 2, 8, 8, 4, 2, 2, 6, 8, 18, 24, 12, 16, 1, 2, 7, 8, 8, 1)],
+        in_specs=[VM] * 7,
+        out_specs=[VM] * 5,
+        scratch_shapes=[pltpu.VMEM((WIDE, TOK), BF), pltpu.VMEM((8, TOK), BF)]
+        + [pltpu.VMEM(*b) for b in PRE_BUFFERS]
+        + [DMA((n,)) for n in PRE_SEMS]
+        + [pltpu.VMEM(*b) for b in COMBINE_BUFFERS]
+        + [DMA((n,)) for n in COMBINE_SEMS],
         compiler_params=pltpu.CompilerParams(
-            collective_id=1, has_side_effects=True, vmem_limit_bytes=60 * 1024 * 1024
+            collective_id=0, has_side_effects=True, vmem_limit_bytes=60 * 1024 * 1024
         ),
-    )(lt, rights)
+    )(*operands)
 
 
 STEP = 512
@@ -808,10 +840,9 @@
 ):
     feats = jnp.transpose(activations, (0, 2, 1))
     old = jnp.transpose(old_factors[0].astype(BF))
-    lt, rights, ids, norms = precondition(
+    AO, EB, router, ids, norms = update(
         feats, old, router_grad, token_ids[None, :], norm_terms, old_router_factor, old_norm_diag
     )
-    AO, EB, router = combine(lt, rights)
     attn, embed, router, norms = finish(AO, EB, router, ids, norms, old_embed_diag[None, :])
     return jnp.transpose(attn, (0, 2, 1)), router, norms, jnp.transpose(embed)
 

time: 212 us -> 195 us (0.920)
  Pallas kernels: 207 us -> 190 us
    pallas_call x2 -> x1, Pallas kernels: 201 us -> 183 us  [update(): pl.pallas_call(update_kernel, out_shape=(jax.ShapeDtypeStruct((4, HALF, W...]
where the time goes in v3:
time: 195 us; the launch traced here: 194 us
  Pallas kernels  190 us (97%)
    pallas_call x1, Pallas kernels, update(): pl.pallas_call(update_kernel, out_shape=(jax.ShapeDtypeStruct((4, HALF, W...  183 us
    pallas_call x1, Pallas kernels, finish(): pl.pallas_call(finish_kernel, grid=(4,), out_shape=(jax.ShapeDtypeStruct(...  6.61 us

profile of v3, /device:TPU:120, one launch (start us, length us, event | category | flops | bytes accessed | tf_op | source)
XLA Modules:
  0.0 194.2 jit_solution(17697823444018546746)
XLA Ops:
  0.6 1.6 copy.12.refs_4_
  2.3 1.9 convert_bitcast_fusion.refs_1_
  4.2 183.5 %shard_map.111 = (bf16[4,288,576]{2,1,0:T(8,128)(2,1)}, bf16[4,2,288,256]{3,2,1,0:T(8,128)(2,1)}, f32[8,576]{1,0:T(8,128)}, f32[8,256]{1,0:T(8,128)}, f32[2,72]{1,0:T(2,128)}) custom-call(bf16[8,72,256]{2,1,0:T(8,128)(2,1)} %bitcast.9, bf16[288,576]{1,0:T(8,128)(2,1)} %convert_bitcast_fusion.refs_1_, bf16[8,256]{1,0:T(8,128)(2,1)} %refs_2_.1, ...), custom_call_target="tpu_custom_call" | custom-call | tf_op jit(solution)/shard_map/pallas_call | solution.py:757
  187.6 6.6 %shard_map.112 = (f32[4,288,576]{2,1,0:T(8,128)}, f32[288,2048]{1,0:T(8,128)}, f32[8,576]{1,0:T(8,128)}, f32[2,72]{1,0:T(2,128)}) custom-call(bf16[4,288,576]{2,1,0:T(8,128)(2,1)} %get-tuple-element.13.AO, bf16[4,2,288,256]{3,2,1,0:T(8,128)(2,1)} %get-tuple-element.14.EB, f32[8,576]{1,0:T(8,128)} %get-tuple-element.15.router_in, ...), custom_call_target="tpu_custom_call" | custom-call | tf_op jit(solution)/shard_map/pallas_call | solution.py:805
